TPU v7x, 32 devices: a whole 2x2x4 slice. The times are simulated.
32 devices in a mesh: var: 4 (over y, x), patch: 8 (over z, core).
Axes of the slice: x: 2, y: 2, z: 4, core: 2. Of those that a mesh axis runs over, the one named last changes fastest.
Arguments:
- field_patches: bfloat16 [48, 4, 8, 2048], P('var', None, 'patch'), may hold values from -6 to 6
- var_ids: int32 [48], replicated, may hold values from 0 to 47, each once
- lead_bucket: int32 [8], P('patch'), may hold values from 0 to 7
- patch_weight: bfloat16 [48, 4, 1024], P('var'), may hold values from -3 to 3
- var_embed: bfloat16 [48, 1024], replicated, may hold values from -6 to 6
- agg_query: bfloat16 [1024], replicated, may hold values from -6 to 6
- agg_key: bfloat16 [1024, 1024], replicated, may hold values from -0.1875 to 0.1875
- agg_value: bfloat16 [1024, 1024], replicated, may hold values from -0.1875 to 0.1875
- agg_out: bfloat16 [1024, 1024], replicated, may hold values from -0.375 to 0.375
- lead_table: bfloat16 [8, 1024], replicated, may hold values from -3 to 3
- ln1_gain: bfloat16 [1024], replicated, may hold values from 0.099609375 to 1.8984375
- attn_qkv: bfloat16 [1024, 3072], replicated, may hold values from -0.25 to 0.25
- attn_out: bfloat16 [1024, 1024], replicated, may hold values from -1.5 to 1.5
- ln2_gain: bfloat16 [1024], replicated, may hold values from 0.099609375 to 1.8984375
- mlp_in: bfloat16 [1024, 4096], replicated, may hold values from -0.1875 to 0.1875
- mlp_in_bias: bfloat16 [4096], replicated, may hold values from -3 to 3
- mlp_out: bfloat16 [4096, 1024], replicated, may hold values from -0.125 to 0.125
- cotangent: bfloat16 [8, 2048, 1024], P('patch', 'var'), may hold values from -6 to 6
Outputs:
- output: bfloat16 [8, 2048, 1024], P('patch', 'var')
- field_grad: float32 [48, 4, 8, 2048], P('var', None, 'patch')
- patch_weight_grad: float32 [48, 4, 1024], P('var')
- var_embed_grad: float32 [48, 1024], P('var')
- agg_query_grad: float32 [1024], P('var')
- agg_key_grad: float32 [1024, 1024], P('var')
- agg_value_grad: float32 [1024, 1024], P('var')
- agg_out_grad: float32 [1024, 1024], P('var')
- lead_table_grad: float32 [8, 1024], P('var')
- ln1_gain_grad: float32 [1024], P('var')
- attn_qkv_grad: float32 [1024, 3072], P('var')
- attn_out_grad: float32 [1024, 1024], P('var')
- ln2_gain_grad: float32 [1024], P('var')
- mlp_in_grad: float32 [1024, 4096], P('var')
- mlp_in_bias_grad: float32 [4096], P('var')
- mlp_out_grad: float32 [4096, 1024], P('var')
Inputs may be any that keep to these rules, and one draw needn't show every extreme that they name: var_ids names each of the 48 variables once.
All inputs are finite; a program needn't handle non-finite values.
Results may differ from a plain program's by a relative error of at most 0.02.
Values may be sent and summed in bfloat16 or wider, within the bound.
No kernel may reach another device: no remote copies, remote signals or barrier semaphores. Data moves between devices by JAX's collectives and lax.ppermute only.
A program may use at most 256 MiB of HBM per device.

v0:
```python
from functools import partial

import jax
import jax.numpy as jnp
from jax import lax
from jax.experimental import pallas as pl
from jax.experimental.pallas import tpu as pltpu
from jax.sharding import Mesh
from jax.sharding import PartitionSpec as P

HEADS = 16
PIX = 4
HEAD_DIM = 64
LEADS = 8
FREE = 4
ORDER = (0, 2, 1, 3)
BLOCKS = tuple((k, 0) for k in range(4)) + tuple((k, 1) for k in ORDER)

f32, bf16 = jnp.float32, jnp.bfloat16
highest = lax.Precision.HIGHEST
epsilon = 1e-05
NT = (((1,), (1,)), ((), ()))
LIGHT = pl.CostEstimate(flops=1, bytes_accessed=1, transcendentals=0)
TN = (((0,), (0,)), ((), ()))


def head_weights(pixels, key_ref, head):
    scores = key_ref[PIX, :, head : head + 1]
    for c in range(PIX):
        scores = scores + pixels[c] * key_ref[c, :, head : head + 1]
    soft = jnp.exp(scores - jnp.max(scores, axis=0, keepdims=True))
    return soft * (1.0 / jnp.sum(soft, axis=0, keepdims=True))


def slot_spans(member, own):
    return [pl.ds(pl.multiple_of((member[0] ^ k) * own, own), own) for k in ORDER]


def weighted_pixels(soft, pixels):
    return jnp.concatenate(
        [(soft * pixels[c]).astype(bf16) for c in range(PIX)] + [soft.astype(bf16)], axis=0
    )


def prepare_kernel(*refs, groups):
    blocks = refs[:groups]
    pick_ref, embed_ref, query_ref, weight_ref, pixel_ref, key_ref, value_ref, value_t_ref, slot_ref, stacked, by_slot = refs[groups:]
    channels = blocks[0].shape[0]
    seq = pixel_ref.shape[2]
    count = channels * groups
    stride = by_slot.shape[0] // groups
    by_slot[...] = jnp.zeros_like(by_slot)
    embeds = jnp.dot(pick_ref[...], embed_ref[...], preferred_element_type=f32)
    for k, block in enumerate(blocks):
        for c in range(PIX + 1):
            if c < PIX:
                pixel_ref[c, k * channels : (k + 1) * channels, :] = block[:, c, :seq].astype(f32)
                rows = block[:, c, seq:].astype(f32)
            else:
                rows = embeds[k * channels : (k + 1) * channels, :]
            stacked[c * count + k * channels : c * count + (k + 1) * channels, :] = rows
            by_slot[k * stride + c * channels : k * stride + (c + 1) * channels, :] = rows
    slot_ref[...] = by_slot[...].astype(bf16)
    keys = jnp.dot(stacked[...], query_ref[...], precision=highest, preferred_element_type=f32)
    for c in range(PIX + 1):
        key_ref[c] = keys[c * count : (c + 1) * count]
    values = jnp.dot(stacked[...].astype(bf16), weight_ref[...], preferred_element_type=f32).astype(bf16)
    value_ref[...] = values
    value_t_ref[...] = values.T


def prepare(blocks, pick, var_embed, query_keys, agg_value, seq):
    groups = len(blocks)
    channels = blocks[0].shape[0]
    count = channels * groups
    width = agg_value.shape[0]
    rows = (PIX + 1) * count
    deep = rows + FREE * groups
    return pl.pallas_call(
        partial(prepare_kernel, groups=groups),
        out_shape=[
            jax.ShapeDtypeStruct((PIX, count, seq), f32),
            jax.ShapeDtypeStruct((PIX + 1, count, query_keys.shape[1]), f32),
            jax.ShapeDtypeStruct((rows, width), bf16),
            jax.ShapeDtypeStruct((width, rows), bf16),
            jax.ShapeDtypeStruct((deep, width), bf16),
        ],
        scratch_shapes=[pltpu.VMEM((rows, width), f32), pltpu.VMEM((deep, width), f32)],
        cost_estimate=LIGHT,
        name="prepare",
    )(*blocks, pick, var_embed, query_keys, agg_value)


def front_kernel(
    member,
    bucket,
    pixel_ref,
    key_ref,
    value_ref,
    out_ref,
    lead_ref,
    gain_ref,
    wq_ref,
    wk_ref,
    wv_ref,
    hidden_ref,
    qkv_ref,
    resid_ref,
    att_ref,
    att_scratch,
):
    pixels = [pixel_ref[c] for c in range(PIX)]
    for head in range(HEADS):
        soft = head_weights(pixels, key_ref, head)
        span = slice(head * HEAD_DIM, (head + 1) * HEAD_DIM)
        att_scratch[span, :] = jnp.dot(
            value_ref[span, :], weighted_pixels(soft, pixels), preferred_element_type=f32
        ).astype(bf16)
    att = att_scratch[...]
    line = lax.broadcasted_iota(jnp.int32, lead_ref.shape, 0)
    lead = jnp.sum(jnp.where(line == bucket[0], lead_ref[...].astype(f32), 0.0), axis=0, keepdims=True)
    resid = lax.dot_general(att, out_ref[...], TN, preferred_element_type=f32) + lead
    centered = resid - jnp.mean(resid, axis=1, keepdims=True)
    inverse = lax.rsqrt(jnp.mean(centered * centered, axis=1, keepdims=True) + epsilon)
    hidden = (centered * inverse * gain_ref[...]).astype(bf16)
    own = wq_ref.shape[1]
    hidden_ref[...] = hidden.T
    for t, weight in enumerate((wq_ref, wk_ref, wv_ref)):
        qkv_ref[:, t * own : (t + 1) * own] = jnp.dot(
            hidden, weight[...], preferred_element_type=f32
        ).astype(bf16)

    @pl.when(pl.program_id(0) == member[0])
    def _():
        resid_ref[...] = resid
        att_ref[...] = att


def front(member, bucket, pixels, key_rows, values_t, agg_out, lead_table, gain, attn_qkv, groups):
    width = agg_out.shape[0]
    own = width // groups
    channels, seq = pixels.shape[1:]
    rows = seq // groups
    spec = pltpu.PrefetchScalarGridSpec(
        num_scalar_prefetch=2,
        grid=(groups,),
        in_specs=[
            pl.BlockSpec((PIX, channels, rows), lambda i, m, l: (0, 0, i)),
            pl.BlockSpec(key_rows.shape, lambda i, m, l: (0, 0, 0)),
            pl.BlockSpec(values_t.shape, lambda i, m, l: (0, 0)),
            pl.BlockSpec(agg_out.shape, lambda i, m, l: (0, 0)),
            pl.BlockSpec(lead_table.shape, lambda i, m, l: (0, 0)),
            pl.BlockSpec((1, width), lambda i, m, l: (0, 0)),
            pl.BlockSpec((width, own), lambda i, m, l: (0, m[0])),
            pl.BlockSpec((width, own), lambda i, m, l: (0, groups + m[0])),
            pl.BlockSpec((width, own), lambda i, m, l: (0, 2 * groups + m[0])),
        ],
        out_specs=[
            pl.BlockSpec((width, rows), lambda i, m, l: (0, i)),
            pl.BlockSpec((rows, 3 * own), lambda i, m, l: (i, 0)),
            pl.BlockSpec((rows, width), lambda i, m, l: (0, 0)),
            pl.BlockSpec((width, rows), lambda i, m, l: (0, 0)),
        ],
        scratch_shapes=[pltpu.VMEM((width, rows), bf16)],
    )
    return pl.pallas_call(
        front_kernel,
        grid_spec=spec,
        out_shape=[
            jax.ShapeDtypeStruct((width, seq), bf16),
            jax.ShapeDtypeStruct((seq, 3 * own), bf16),
            jax.ShapeDtypeStruct((rows, width), f32),
            jax.ShapeDtypeStruct((width, rows), bf16),
        ],
        cost_estimate=LIGHT,
        name="front",
    )(member, bucket, pixels, key_rows, values_t, agg_out, lead_table, gain, attn_qkv, attn_qkv, attn_qkv)


def attend_kernel(member, q_ref, k_ref, v_ref, mixed_ref, lse_ref):
    rows = q_ref.shape[0]
    lane = lax.broadcasted_iota(jnp.int32, (1, 2 * HEAD_DIM), 1)
    queries = q_ref[...] * jnp.asarray(0.125, bf16)
    mixed = jnp.zeros((rows, 2 * HEAD_DIM), f32)
    seq = k_ref.shape[0]
    for part in range(2):
        keep = (lane // HEAD_DIM) == part
        query = jnp.where(keep, queries, jnp.zeros_like(queries))
        top = total = out = None
        for span in (slice(0, seq // 2), slice(seq // 2, seq)):
            scores = lax.dot_general(query, k_ref[span, :], NT, preferred_element_type=f32)
            peak = jnp.max(scores, axis=1, keepdims=True)
            if top is not None:
                peak = jnp.maximum(peak, top)
            soft = jnp.exp(scores - peak)
            weight = jnp.sum(soft, axis=1, keepdims=True)
            value = jnp.dot(soft.astype(bf16), v_ref[span, :], preferred_element_type=f32)
            if top is None:
                total, out = weight, value
            else:
                scale = jnp.exp(top - peak)
                total, out = total * scale + weight, out * scale + value
            top = peak
        mixed = jnp.where(keep, out * (1.0 / total), mixed)
        lse = jnp.broadcast_to(top + jnp.log(total), (rows, 2 * HEAD_DIM))
        lse_ref[0, part : part + 1, :] = lse.T[0:1, :]
    mixed_ref[...] = mixed.astype(bf16)


def attend(member, qkv, slot, rows, block):
    seq = qkv.shape[0]
    pair = 2 * HEAD_DIM
    pairs = qkv.shape[1] // (3 * pair)
    steps = rows // block
    spec = pltpu.PrefetchScalarGridSpec(
        num_scalar_prefetch=1,
        grid=(pairs, steps),
        in_specs=[
            pl.BlockSpec((block, pair), lambda p, i, m: ((m[0] ^ slot) * steps + i, p)),
            pl.BlockSpec((seq, pair), lambda p, i, m: (0, pairs + p)),
            pl.BlockSpec((seq, pair), lambda p, i, m: (0, 2 * pairs + p)),
        ],
        out_specs=[
            pl.BlockSpec((block, pair), lambda p, i, m: (i, p)),
            pl.BlockSpec((1, 2, block), lambda p, i, m: (p, 0, i)),
        ],
    )
    return pl.pallas_call(
        attend_kernel,
        grid_spec=spec,
        out_shape=[
            jax.ShapeDtypeStruct((rows, pairs * pair), bf16),
            jax.ShapeDtypeStruct((pairs, 2, rows), f32),
        ],
        cost_estimate=LIGHT,
        name="attend",
    )(member, qkv, qkv, qkv)


def attend_back_kernel(member, q_ref, k_ref, v_ref, g_ref, *refs, chunk, groups):
    mixed_refs, lse_refs = refs[:groups], refs[groups : 2 * groups]
    out_ref, dk_acc, dv_acc, kt = refs[2 * groups :]
    i = pl.program_id(0)
    slot = i ^ member[0]
    mixed, lse_rows = mixed_refs[0][...], lse_refs[0][0]
    for k in range(1, groups):
        mixed = jnp.where(slot == k, mixed_refs[k][...], mixed)
        lse_rows = jnp.where(slot == k, lse_refs[k][0], lse_rows)
    block = q_ref.shape[0]
    seq = k_ref.shape[0]
    pair = 2 * HEAD_DIM
    lane = lax.broadcasted_iota(jnp.int32, (1, pair), 1)
    side = lax.broadcasted_iota(jnp.int32, (pair, 1), 0)

    @pl.when(i == 0)
    def _():
        dk_acc[...] = jnp.zeros_like(dk_acc)
        dv_acc[...] = jnp.zeros_like(dv_acc)
        kt[...] = k_ref[...].T

    queries = q_ref[...] * jnp.asarray(0.125, bf16)
    grads = g_ref[...]
    product = (grads.astype(f32) * mixed.astype(f32)).T
    grad_query = jnp.zeros((pair, block), f32)
    for part in range(2):
        keep = (lane // HEAD_DIM) == part
        query = jnp.where(keep, queries, jnp.zeros_like(queries))
        grad = jnp.where(keep, grads, jnp.zeros_like(grads))
        delta = jnp.sum(product[part * HEAD_DIM : (part + 1) * HEAD_DIM], axis=0, keepdims=True)
        lse = lse_rows[part : part + 1, :]
        total = jnp.zeros((pair, block), f32)
        for at in range(0, seq, chunk):
            span = pl.ds(at, chunk)
            scores = lax.dot_general(k_ref[span, :], query, NT, preferred_element_type=f32)
            soft = jnp.exp(scores - lse)
            through = lax.dot_general(v_ref[span, :], grad, NT, preferred_element_type=f32)
            grad_scores = (soft * (through - delta)).astype(bf16)
            dv_acc[span, :] += jnp.dot(soft.astype(bf16), grad, preferred_element_type=f32)
            dk_acc[span, :] += jnp.dot(grad_scores, query, preferred_element_type=f32)
            total += jnp.dot(kt[:, span], grad_scores, preferred_element_type=f32)
        grad_query = jnp.where((side // HEAD_DIM) == part, total, grad_query)
    out_ref[pl.ds(pl.multiple_of(i * block, block), block), 0:pair] = (grad_query.T * 0.125).astype(bf16)

    @pl.when(i == pl.num_programs(0) - 1)
    def _():
        out_ref[:, pair : 2 * pair] = dk_acc[...].astype(bf16)
        out_ref[:, 2 * pair : 3 * pair] = dv_acc[...].astype(bf16)


def attend_back(member, qkv, grads, mixed, lse, which, chunk):
    seq = qkv.shape[0]
    groups = len(mixed)
    rows = seq // groups
    pair = 2 * HEAD_DIM
    pairs = qkv.shape[1] // (3 * pair)
    spec = pltpu.PrefetchScalarGridSpec(
        num_scalar_prefetch=1,
        grid=(groups,),
        in_specs=[
            pl.BlockSpec((rows, pair), lambda i, m: (i, which)),
            pl.BlockSpec((seq, pair), lambda i, m: (0, pairs + which)),
            pl.BlockSpec((seq, pair), lambda i, m: (0, 2 * pairs + which)),
            pl.BlockSpec((rows, pair), lambda i, m: (i, which)),
        ]
        + [pl.BlockSpec((rows, pair), lambda i, m: (0, which))] * groups
        + [pl.BlockSpec((1, 2, rows), lambda i, m: (which, 0, 0))] * groups,
        out_specs=pl.BlockSpec((seq, 3 * pair), lambda i, m: (0, 0)),
        scratch_shapes=[pltpu.VMEM((seq, pair), f32), pltpu.VMEM((seq, pair), f32), pltpu.VMEM((pair, seq), bf16)],
    )
    return pl.pallas_call(
        partial(attend_back_kernel, chunk=min(chunk, seq), groups=groups),
        grid_spec=spec,
        out_shape=jax.ShapeDtypeStruct((seq, 3 * pair), bf16),
        cost_estimate=LIGHT,
        name="attend_back",
    )(member, qkv, qkv, qkv, grads, *mixed, *lse)


def put_tail(tail, values, span):
    groups = len(ORDER)
    channels = values.shape[0] // ((PIX + 1) * groups)
    stride = tail.shape[0] // groups
    for at, k in enumerate(ORDER):
        for c in range(PIX + 1):
            row, source = at * stride + c * channels, (c * groups + k) * channels
            tail[row : row + channels, span] = values[source : source + channels]


def aggregate_back_kernel(
    member, core, bucket, pixel_ref, key_ref, value_ref, grad_ref, bias_ref, gain2_ref, gain1_ref, sum_ref,
    field_ref, keep_ref, send_ref, tail
):
    count, rows = pixel_ref.shape[1:]
    pair = 2 * HEAD_DIM
    pixels = [pixel_ref[c] for c in range(PIX)]
    lane = lax.broadcasted_iota(jnp.int32, (1, pair), 1)
    side = lax.broadcasted_iota(jnp.int32, (pair, 1), 0)
    field = [jnp.zeros((count, rows), f32) for _ in range(PIX)]
    keys = [jnp.zeros((count, pair), f32) for _ in range(PIX + 1)]
    for which in range(HEADS // 2):
        span = slice(which * pair, (which + 1) * pair)
        values, grads = value_ref[:, span], grad_ref[span, :]
        total = jnp.zeros(((PIX + 1) * count, pair), f32)
        for part in range(2):
            head = which * 2 + part
            grad = jnp.where((side // HEAD_DIM) == part, grads, jnp.zeros_like(grads))
            through = jnp.dot(values, grad, preferred_element_type=f32)
            kinds = [through[c * count : (c + 1) * count] for c in range(PIX + 1)]
            soft = head_weights(pixels, key_ref, head)
            grad_soft = kinds[PIX]
            for c in range(PIX):
                grad_soft = grad_soft + pixels[c] * kinds[c]
            weighed = soft * grad_soft
            grad_scores = weighed - soft * jnp.sum(weighed, axis=0, keepdims=True)
            for c in range(PIX):
                field[c] = field[c] + soft * kinds[c] + grad_scores * key_ref[c, :, head : head + 1]
                keys[c] = jnp.where(lane == head, jnp.sum(grad_scores * pixels[c], axis=1, keepdims=True), keys[c])
            keys[PIX] = jnp.where(lane == head, jnp.sum(grad_scores, axis=1, keepdims=True), keys[PIX])
            total = total + lax.dot_general(weighted_pixels(soft, pixels), grad, NT, preferred_element_type=f32)
        put_tail(tail, total, span)
    for c in range(PIX):
        field_ref[c] = field[c].astype(bf16)
    width = value_ref.shape[1]
    put_tail(tail, jnp.concatenate(keys, axis=0), slice(width, width + pair))
    groups = len(ORDER)
    stride = tail.shape[0] // groups
    own, lines = width // groups, LEADS // groups
    for at, k in enumerate(ORDER):
        owner = member[0] ^ k
        start = (at + 1) * stride - FREE
        tail[start : start + FREE, :] = jnp.zeros((FREE, tail.shape[1]), f32)
        tail[start : start + 1, :width] = bias_ref[:, pl.ds(pl.multiple_of(owner * width, width), width)]
        chunk = pl.ds(pl.multiple_of(owner * own, own), own)
        tail[start + 1 : start + 2, :own] = gain2_ref[:, chunk]
        tail[start + 1 : start + 2, own : 2 * own] = gain1_ref[:, chunk]
        for line in range(lines):
            hit = bucket[0] == owner * lines + line
            tail[start + 2 + line : start + 3 + line, :width] = jnp.where(hit, sum_ref[...], 0.0)
    half = width // 2
    for ref, which in ((keep_ref, core[0]), (send_ref, 1 - core[0])):
        ref[:, :half] = tail[:, pl.ds(pl.multiple_of(which * half, half), half)].astype(bf16)
        ref[:, half:] = tail[:, width:].astype(bf16)


def aggregate_back(member, core, bucket, pixels, key_rows, values, grads, small, groups):
    count, seq = pixels.shape[1:]
    rows = seq // groups
    width = values.shape[1]
    deep = (PIX + 1) * count + FREE * groups
    wide = width // 2 + 2 * HEAD_DIM

    def whole(*shape):
        return pl.BlockSpec(shape, lambda i, *_: (0,) * len(shape))

    spec = pltpu.PrefetchScalarGridSpec(
        num_scalar_prefetch=3,
        grid=(1,),
        in_specs=[
            pl.BlockSpec((PIX, count, rows), lambda i, m, c, l: (0, 0, m[0])),
            whole(*key_rows.shape),
            whole(*values.shape),
            whole(*grads.shape),
            *[whole(*value.shape) for value in small],
        ],
        out_specs=[whole(PIX, count, rows), whole(deep, wide), whole(deep, wide)],
        scratch_shapes=[pltpu.VMEM((deep, width + 2 * HEAD_DIM), f32)],
    )
    return pl.pallas_call(
        aggregate_back_kernel,
        grid_spec=spec,
        out_shape=[
            jax.ShapeDtypeStruct((PIX, count, rows), bf16),
            jax.ShapeDtypeStruct((deep, wide), bf16),
            jax.ShapeDtypeStruct((deep, wide), bf16),
        ],
        cost_estimate=LIGHT,
        name="aggregate_back",
    )(member, core, bucket, pixels, key_rows, values, grads, *small)


def shape_of(*dims, kind=bf16):
    return jax.ShapeDtypeStruct(dims, kind)


def inner_kernel(
    member, core, mixed0, mixed1, mixed2, mixed3, wo_ref, resid_ref, gain_ref, w1_ref, b1_ref, ga_ref,
    act_ref, act_t_ref, send_ref, keep_ref, bias_ref, one_ref, hidden_ref, mixed_ref, hidden,
):
    j = pl.program_id(0)
    parts = (mixed0, mixed1, mixed2, mixed3)
    rows, own = mixed0.shape

    @pl.when(j == 0)
    def _():
        resid = resid_ref[...]
        for slot, part in enumerate(parts):
            owner = pl.ds(pl.multiple_of((member[0] ^ slot) * own, own), own)
            resid = resid + jnp.dot(part[...], wo_ref[owner, :], preferred_element_type=f32)
        one_ref[...] = resid
        centered = resid - jnp.mean(resid, axis=1, keepdims=True)
        scale = lax.rsqrt(jnp.mean(centered * centered, axis=1, keepdims=True) + epsilon)
        hidden[...] = (centered * scale * gain_ref[...]).astype(bf16)
        piece = own // 2
        for at, (slot, side) in enumerate(BLOCKS):
            start = pl.multiple_of((member[0] ^ slot) * own + side * piece, piece)
            hidden_ref[at * piece : (at + 1) * piece, :] = hidden[:, pl.ds(start, piece)].T
            mixed_ref[at * piece : (at + 1) * piece, :] = parts[slot][:, side * piece : (side + 1) * piece].T

    inner = jnp.dot(hidden[...], w1_ref[...], preferred_element_type=f32) + b1_ref[...]
    below = 0.5 + 0.5 * lax.erf(inner * 0.7071067811865476)
    act = (inner * below).astype(bf16)
    slope = below + inner * (jnp.exp(-0.5 * inner * inner) * 0.3989422804014327)
    gu = (slope * ga_ref[...].astype(f32)).astype(bf16)
    act_ref[...] = act
    act_t_ref[...] = act.T
    bias_ref[...] = jnp.sum(gu.astype(f32), axis=0, keepdims=True)

    @pl.when(j < len(parts))
    def _():
        send_ref[...] = gu

    @pl.when(j >= len(parts))
    def _():
        keep_ref[...] = gu


def inner_part(member, core, mixed, attn_out, resid, gain, mlp_in, bias, grad_act):
    rows, width = resid.shape
    inner = mlp_in.shape[1]
    groups = len(mixed)
    own = width // groups
    steps = 2 * groups
    block = inner // steps

    def natural(j, c):
        return ((j // groups) ^ (1 - c[0])) * groups + j % groups

    def spot(j, m, c):
        n = natural(j, c)
        slot = (n // 2) ^ m[0]
        return (jnp.where(n % 2 == 0, slot, 4 + (slot % 2) * 2 + slot // 2), 0)

    def whole(*shape):
        return pl.BlockSpec(shape, lambda j, m, c: (0,) * len(shape))

    def column(deep):
        return pl.BlockSpec((deep, block), lambda j, m, c: (0, natural(j, c)))

    spec = pltpu.PrefetchScalarGridSpec(
        num_scalar_prefetch=2,
        grid=(steps,),
        in_specs=[whole(rows, own)] * groups
        + [whole(width, width), whole(rows, width), whole(1, width)]
        + [column(width), column(1), column(rows)],
        out_specs=[
            column(rows),
            pl.BlockSpec((block, rows), spot),
            pl.BlockSpec((rows, block), lambda j, m, c: (0, jnp.minimum(j, groups - 1))),
            pl.BlockSpec((rows, block), lambda j, m, c: (0, jnp.maximum(j - groups, 0))),
            column(1),
            whole(rows, width),
            whole(width, rows),
            whole(width, rows),
        ],
        scratch_shapes=[pltpu.VMEM((rows, width), bf16)],
    )
    return pl.pallas_call(
        inner_kernel,
        grid_spec=spec,
        out_shape=[shape_of(rows, inner), shape_of(inner, rows)]
        + [shape_of(rows, inner // 2)] * 2
        + [shape_of(1, inner, kind=f32), shape_of(rows, width, kind=f32)]
        + [shape_of(width, rows)] * 2,
        cost_estimate=LIGHT,
        name="inner_part",
    )(member, core, *mixed, attn_out, resid, gain, mlp_in, bias, grad_act)


def outer_kernel(
    core, act_ref, send_ref, keep_ref, w1_ref, w2_ref, wo_ref, one_ref, gain_ref, g_ref,
    out_ref, gres_ref, gb_ref, gb_send_ref, gm_ref, ggain_ref, branch, grads,
):
    j = pl.program_id(0)
    groups, rows, own = gm_ref.shape
    half = send_ref.shape[1]
    branch[j] = jnp.dot(act_ref[...], w2_ref[...], preferred_element_type=f32)

    def columns(which):
        return w1_ref[:, pl.ds(pl.multiple_of(which * half, half), half)]

    grads[j] = lax.dot_general(
        send_ref[...], columns(1 - core[0]), NT, preferred_element_type=f32
    ) + lax.dot_general(keep_ref[...], columns(core[0]), NT, preferred_element_type=f32)

    @pl.when(j == pl.num_programs(0) - 1)
    def _():
        count = branch.shape[0]
        resid = one_ref[...]
        out_ref[...] = (resid + jnp.concatenate([branch[i] for i in range(count)], axis=1)).astype(bf16)
        centered = resid - jnp.mean(resid, axis=1, keepdims=True)
        scale = lax.rsqrt(jnp.mean(centered * centered, axis=1, keepdims=True) + epsilon)
        grad, plain = jnp.concatenate([grads[i] for i in range(count)], axis=1), centered * scale
        ggain_ref[...] = jnp.sum(grad * plain, axis=0, keepdims=True)
        grad = grad * gain_ref[...]
        first = jnp.mean(grad, axis=1, keepdims=True)
        second = jnp.mean(grad * plain, axis=1, keepdims=True)
        gres = g_ref[...].astype(f32) + scale * (grad - first - plain * second)
        gres_ref[...] = gres
        gb_ref[...] = gres.astype(bf16)
        width = gb_ref.shape[1]
        gb_send_ref[...] = gb_ref[:, pl.ds(pl.multiple_of((1 - core[0]) * (width // 2), width // 2), width // 2)]
        gb = gb_ref[...]
        for p in range(groups):
            gm_ref[p] = lax.dot_general(gb, wo_ref[p * own : (p + 1) * own, :], NT, preferred_element_type=f32).astype(
                bf16
            )


def outer_part(core, act, gu_send, gu_keep, mlp_in, mlp_out, attn_out, resid, gain, grad_out, groups):
    rows, width = resid.shape
    inner = mlp_in.shape[1]
    own = width // groups
    steps = 4
    block = width // steps

    def whole(*shape):
        return pl.BlockSpec(shape, lambda j, c: (0,) * len(shape))

    spec = pltpu.PrefetchScalarGridSpec(
        num_scalar_prefetch=1,
        grid=(steps,),
        in_specs=[
            whole(rows, inner),
            whole(rows, inner // 2),
            whole(rows, inner // 2),
            pl.BlockSpec((block, inner), lambda j, c: (j, 0)),
            pl.BlockSpec((inner, block), lambda j, c: (0, j)),
            whole(width, width),
            whole(rows, width),
            whole(1, width),
            whole(rows, width),
        ],
        out_specs=[
            whole(rows, width),
            whole(rows, width),
            whole(rows, width),
            whole(rows, width // 2),
            whole(groups, rows, own),
            whole(1, width),
        ],
        scratch_shapes=[pltpu.VMEM((steps, rows, block), f32), pltpu.VMEM((steps, rows, block), f32)],
    )
    return pl.pallas_call(
        outer_kernel,
        grid_spec=spec,
        out_shape=[
            shape_of(rows, width),
            shape_of(rows, width, kind=f32),
            shape_of(rows, width),
            shape_of(rows, width // 2),
            shape_of(groups, rows, own),
            shape_of(1, width, kind=f32),
        ],
        cost_estimate=LIGHT,
        name="outer_part",
    )(core, act, gu_send, gu_keep, mlp_in, mlp_out, attn_out, resid, gain, grad_out)


def both_dots(left, left_other, right, right_other):
    return jnp.dot(left[...], right[...], preferred_element_type=f32) + jnp.dot(
        left_other[...], right_other[...], preferred_element_type=f32
    )


def out_grad_kernel(core, left, left_other, right, right_other, *outs):
    total = both_dots(left, left_other, right, right_other).astype(bf16)
    for q, out in enumerate(outs):

        @pl.when(pl.program_id(0) == q)
        def _():
            out[...] = total


def out_grad(core, left, left_other, right, right_other):
    rows, deep = left.shape
    half = right.shape[1] // 2
    block = rows // 4

    spec = pltpu.PrefetchScalarGridSpec(
        num_scalar_prefetch=1,
        grid=(4,),
        in_specs=[pl.BlockSpec((block, deep), lambda i, c: (i, 0))] * 2
        + [
            pl.BlockSpec((deep, half), lambda i, c: (0, c[0])),
            pl.BlockSpec((deep, half), lambda i, c: (0, 0)),
        ],
        out_specs=[pl.BlockSpec((block, half), lambda i, c: (0, 0)) for q in range(4)],
    )
    return pl.pallas_call(
        out_grad_kernel,
        grid_spec=spec,
        out_shape=[shape_of(rows // 4, half)] * 4,
        cost_estimate=LIGHT,
        name="out_grad",
    )(core, left, left_other, right, right_other)


def in_grad_kernel(core, high, h, h_other, u, u_other, m, m_other, b, b_other, keep, send):
    units = u.shape[1]

    def put(out):
        out[:, :units] = both_dots(h, h_other, u, u_other).astype(bf16)
        out[:, units:] = both_dots(m, m_other, b, b_other).astype(bf16)

    @pl.when(pl.program_id(0) == 0)
    def _():
        put(send)

    @pl.when(pl.program_id(0) == 1)
    def _():
        put(keep)


def in_grad(core, high, h, h_other, u, u_other, m, m_other, b, b_other):
    rows, deep = h.shape
    units, branch = u.shape[1] // 2, b_other.shape[1] // 2

    def whole(*shape):
        return pl.BlockSpec(shape, lambda i, c, z: (0,) * len(shape))

    def side(i, c, z):
        return (0, z[0] ^ (1 - i))

    def core_side(i, c, z):
        return (0, 2 * c[0] + (z[0] ^ (1 - i)))

    spec = pltpu.PrefetchScalarGridSpec(
        num_scalar_prefetch=2,
        grid=(2,),
        in_specs=[
            whole(rows, deep),
            whole(rows, deep),
            pl.BlockSpec((deep, units), side),
            pl.BlockSpec((deep, units), side),
            whole(rows, deep),
            whole(rows, deep),
            pl.BlockSpec((deep, branch), core_side),
            pl.BlockSpec((deep, branch), side),
        ],
        out_specs=[whole(rows, units + branch)] * 2,
    )
    return pl.pallas_call(
        in_grad_kernel,
        grid_spec=spec,
        out_shape=[shape_of(rows, units + branch)] * 2,
        cost_estimate=LIGHT,
        name="in_grad",
    )(core, high, h, h_other, u, u_other, m, m_other, b, b_other)


def qkv_grad_kernel(core, h, h_other, *refs):
    out = refs[-1]
    for which in range(2):

        @pl.when(core[0] == which)
        def _():
            out[...] = both_dots(h, h_other, refs[which], refs[2 + which]).astype(bf16)


def qkv_grad(core, h, h_other, grads, others):
    rows, deep = h.shape
    cols = grads[0].shape[1]
    block = rows // 2
    spec = pltpu.PrefetchScalarGridSpec(
        num_scalar_prefetch=1,
        grid=(2,),
        in_specs=[pl.BlockSpec((block, deep), lambda i, c: (i, 0))] * 2
        + [pl.BlockSpec((deep, cols), lambda i, c: (0, 0))] * 4,
        out_specs=pl.BlockSpec((block, cols), lambda i, c: (i, 0)),
    )
    return pl.pallas_call(
        qkv_grad_kernel,
        grid_spec=spec,
        out_shape=shape_of(rows, cols),
        cost_estimate=LIGHT,
        name="qkv_grad",
    )(core, h, h_other, *grads, *others)


def last_grad_kernel(core, qkv_ref, a, a_other, g, g_other, out):
    cols = qkv_ref.shape[1]
    out[0, :, :cols] = qkv_ref[...]
    out[0, :, cols:] = both_dots(a, a_other, g, g_other).astype(bf16)


def last_grad(core, weight_qkv, att, att_other, grad, grad_other, groups):
    rows, deep = att.shape
    half = grad_other.shape[1]
    cols = weight_qkv.shape[1]
    block = rows // groups
    spec = pltpu.PrefetchScalarGridSpec(
        num_scalar_prefetch=1,
        grid=(groups,),
        in_specs=[
            pl.BlockSpec((block, cols), lambda i, c: (i, 0)),
            pl.BlockSpec((block, deep), lambda i, c: (i, 0)),
            pl.BlockSpec((block, deep), lambda i, c: (i, 0)),
            pl.BlockSpec((deep, half), lambda i, c: (0, c[0])),
            pl.BlockSpec((deep, half), lambda i, c: (0, 0)),
        ],
        out_specs=pl.BlockSpec((1, block, cols + half), lambda i, c: (i, 0, 0)),
    )
    return pl.pallas_call(
        last_grad_kernel,
        grid_spec=spec,
        out_shape=shape_of(groups, block, cols + half),
        cost_estimate=LIGHT,
        name="last_grad",
    )(core, weight_qkv, att, att_other, grad, grad_other)


def join_kernel(core, first_ref, second_ref, wq, wk, wv, resid_ref, gain_ref, gres_ref, out_ref, *refs):
    ga_ref, ga_send_ref, gatt_ref, ggain_ref, sum_ref, total = refs
    i = pl.program_id(0)
    pair = 2 * HEAD_DIM

    @pl.when(i == 0)
    def _():
        total[...] = jnp.zeros_like(total)

    spans = [slice(t * pair, (t + 1) * pair) for t in range(3)]
    left = jnp.concatenate([ref[:, span] for span in spans for ref in (first_ref, second_ref)], axis=1)
    weights = jnp.concatenate([wq[...], wk[...], wv[...]], axis=1)
    total[...] += lax.dot_general(left, weights, NT, preferred_element_type=f32)

    @pl.when(i == pl.num_programs(0) - 1)
    def _():
        resid = resid_ref[...]
        centered = resid - jnp.mean(resid, axis=1, keepdims=True)
        scale = lax.rsqrt(jnp.mean(centered * centered, axis=1, keepdims=True) + epsilon)
        plain = centered * scale
        grad = total[...]
        ggain_ref[...] = jnp.sum(grad * plain, axis=0, keepdims=True)
        grad = grad * gain_ref[...]
        first = jnp.mean(grad, axis=1, keepdims=True)
        second = jnp.mean(grad * plain, axis=1, keepdims=True)
        gres = gres_ref[...] + scale * (grad - first - plain * second)
        sum_ref[...] = jnp.sum(gres, axis=0, keepdims=True)
        ga = gres.astype(bf16)
        ga_ref[...] = ga
        half = ga_send_ref.shape[1]
        ga_send_ref[...] = ga_ref[:, pl.ds(pl.multiple_of((1 - core[0]) * half, half), half)]
        gatt_ref[...] = lax.dot_general(out_ref[...], ga, NT, preferred_element_type=f32).astype(bf16)


def join(core, first, second, attn_qkv, resid, gain, gres, agg_out):
    rows, width = resid.shape
    groups = first.shape[0] // rows
    own = width // groups
    cols = first.shape[1]

    def whole(*shape):
        return pl.BlockSpec(shape, lambda i, c: (0,) * len(shape))

    spec = pltpu.PrefetchScalarGridSpec(
        num_scalar_prefetch=1,
        grid=(groups,),
        in_specs=[
            pl.BlockSpec((rows, cols), lambda i, c: (i, 0)),
            pl.BlockSpec((rows, cols), lambda i, c: (i, 0)),
            pl.BlockSpec((width, own), lambda i, c: (0, i)),
            pl.BlockSpec((width, own), lambda i, c: (0, groups + i)),
            pl.BlockSpec((width, own), lambda i, c: (0, 2 * groups + i)),
            whole(rows, width),
            whole(1, width),
            whole(rows, width),
            whole(width, width),
        ],
        out_specs=[
            whole(rows, width),
            whole(rows, width // 2),
            whole(width, rows),
            whole(1, width),
            whole(1, width),
        ],
        scratch_shapes=[pltpu.VMEM((rows, width), f32)],
    )
    return pl.pallas_call(
        join_kernel,
        grid_spec=spec,
        out_shape=[
            shape_of(rows, width),
            shape_of(rows, width // 2),
            shape_of(width, rows),
            shape_of(1, width, kind=f32),
            shape_of(1, width, kind=f32),
        ],
        cost_estimate=LIGHT,
        name="join",
    )(core, first, second, attn_qkv, attn_qkv, attn_qkv, resid, gain, gres, agg_out)


def add(a, b):
    return (a.astype(f32) + b.astype(f32)).astype(bf16)


def split_add(a, b, count):
    deep = a.shape[0] // count
    return [add(a[i * deep : (i + 1) * deep], b[i * deep : (i + 1) * deep]) for i in range(count)]


def pick_add(a, b, which, axis):
    half = a.shape[axis] // 2
    return add(
        lax.dynamic_slice_in_dim(a, which * half, half, axis), lax.dynamic_slice_in_dim(b, which * half, half, axis)
    )


def whole_blocks(shapes):
    return [pl.BlockSpec(shape, lambda i, *_, n=len(shape): (0,) * n) for shape in shapes]


def choose_kernel(high, a, b, c, d, keep, send):
    for value, (first, second) in enumerate(((keep, send), (send, keep))):

        @pl.when(high[0] == value)
        def _():
            first[...] = add(a[...], b[...])
            second[...] = add(c[...], d[...])


def choose(high, a, b, c, d):
    rows, cols = a.shape
    block = pl.BlockSpec((rows // 2, cols), lambda i, z: (i, 0))
    return pl.pallas_call(
        choose_kernel,
        grid_spec=pltpu.PrefetchScalarGridSpec(
            num_scalar_prefetch=1, grid=(2,), in_specs=[block] * 4, out_specs=[block] * 2
        ),
        out_shape=[jax.ShapeDtypeStruct(a.shape, bf16)] * 2,
        cost_estimate=LIGHT,
        name="choose",
    )(high, a, b, c, d)


def gather_sources_kernel(high, came_ref, keep, send, *, cols):
    groups, half = came_ref.shape[0], keep.shape[0]
    for out, which in ((keep, high[0]), (send, 1 - high[0])):
        span = pl.ds(pl.multiple_of(which * half, half), half)
        total = jnp.zeros((half, came_ref.shape[2] - cols), f32)
        for p in range(groups):
            out[:, p * cols : (p + 1) * cols] = came_ref[p, span, :cols]
            total = total + came_ref[p, span, cols:].astype(f32)
        out[:, groups * cols :] = total.astype(bf16)


def gather_sources(high, came, cols):
    groups, rows, wide = came.shape
    shape = (rows // 2, groups * cols + wide - cols)
    spec = pltpu.PrefetchScalarGridSpec(
        num_scalar_prefetch=1, grid=(1,), in_specs=whole_blocks([came.shape]), out_specs=whole_blocks([shape] * 2)
    )
    return pl.pallas_call(
        partial(gather_sources_kernel, cols=cols),
        grid_spec=spec,
        out_shape=[jax.ShapeDtypeStruct(shape, bf16)] * 2,
        cost_estimate=LIGHT,
        name="gather_sources",
    )(high, came)


def turned(i, levels):
    total = 0
    for k in range(levels):
        total = total + (((i >> k) & 1) << (levels - 1 - k))
    return total


def assemble_kernel(where, *refs, order, levels, spans, low_rows):
    pieces, outs = refs[:4], refs[4:]
    deep = pieces[0].shape[0] // len(order)
    for number, ref in enumerate(pieces):
        core = where[1] if number < 2 else 1 - where[1]
        for at, bits in enumerate(order):
            chip = where[0] ^ (bits ^ (number % 2))
            low = low_bit(chip, levels)
            row = turned(chip >> 1, levels - 1)
            if low_rows:
                row = row + (low << (levels - 1))
            to = pl.ds(pl.multiple_of(row * deep, deep), deep)
            for out, source, size, base, by_core, by_low in spans:
                column = pl.multiple_of(base + core * by_core + low * by_low, 128)
                outs[out][to, pl.ds(column, size)] = ref[at * deep : (at + 1) * deep, source : source + size].astype(f32)


def assemble(where, pieces, levels, spans, widths, low_rows=True):
    order = [0]
    for bit in range(levels - 1, 0, -1):
        order = order + [bits ^ (3 if mirrored(levels) else 1 << bit) for bits in order]
    rows = pieces[0].shape[0] * (2 if low_rows else 1)
    shapes = [(rows, wide) for wide in widths]
    spec = pltpu.PrefetchScalarGridSpec(
        num_scalar_prefetch=1,
        grid=(1,),
        in_specs=whole_blocks([p.shape for p in pieces]),
        out_specs=whole_blocks(shapes),
    )
    return pl.pallas_call(
        partial(assemble_kernel, order=tuple(order), levels=levels, spans=tuple(spans), low_rows=low_rows),
        grid_spec=spec,
        out_shape=[shape_of(*shape, kind=f32) for shape in shapes],
        cost_estimate=LIGHT,
        name="assemble",
    )(where, *pieces)


def field_kernel(member, *refs):
    pieces, out = refs[:-1], refs[-1]
    kinds, channels, rows = pieces[0].shape
    for k, piece in enumerate(pieces):
        at = pl.ds(pl.multiple_of((member[0] ^ k) * rows, rows), rows)
        for c in range(kinds):
            out[:, c, at] = piece[c].astype(f32)


def place_field(member, pieces):
    kinds, channels, rows = pieces[0].shape
    shape = (channels, kinds, rows * len(pieces))
    spec = pltpu.PrefetchScalarGridSpec(
        num_scalar_prefetch=1,
        grid=(1,),
        in_specs=whole_blocks([p.shape for p in pieces]),
        out_specs=whole_blocks([shape])[0],
    )
    return pl.pallas_call(
        field_kernel, grid_spec=spec, out_shape=jax.ShapeDtypeStruct(shape, f32), name="place_field"
    )(member, *pieces)


def tail_kernel(member, *refs, groups):
    tails = refs[:groups]
    stacked_ref, pick_ref, value_ref, qk_ref, key_ref, query_ref = refs[groups : groups + 6]
    gvalue_ref, gkey_ref, gquery_ref, patch_ref, table_ref, gqk = refs[groups + 6 :]
    width = value_ref.shape[0]
    own = gvalue_ref.shape[0]
    at = pl.ds(pl.multiple_of(member[0] * own, own), own)
    tail = jnp.concatenate([t[...] for t in tails], axis=0)
    values, keys = tail[:, :width], tail[:, width:]
    gvalue_ref[...] = lax.dot_general(stacked_ref[:, at], values, TN, preferred_element_type=f32)
    gqk[...] = lax.dot_general(stacked_ref[...], keys, TN, preferred_element_type=f32)
    head = lax.broadcasted_iota(jnp.int32, (keys.shape[1], width), 0)
    column = lax.broadcasted_iota(jnp.int32, (keys.shape[1], width), 1) // HEAD_DIM
    spread = jnp.where(head == column, 1.0, 0.0)
    gkey_ref[...] = (
        jnp.dot(gqk[at, :], spread, precision=highest, preferred_element_type=f32) * (query_ref[...] * 0.125)
    )
    by_head = lax.dot_general(gqk[...], key_ref[...].astype(f32), TN, precision=highest, preferred_element_type=f32)
    head = lax.broadcasted_iota(jnp.int32, by_head.shape, 0)
    column = (lax.broadcasted_iota(jnp.int32, by_head.shape, 1) + member[0] * own) // HEAD_DIM
    gquery_ref[...] = jnp.sum(jnp.where(head == column, by_head, 0.0), axis=0, keepdims=True) * 0.125
    own_rows = tails[0].shape[0]
    table = jnp.dot(pick_ref[...], tail, preferred_element_type=f32).astype(bf16)
    rows = jnp.concatenate([tail[:own_rows], table], axis=0)
    total = lax.dot_general(rows[:, :width], value_ref[...], NT, preferred_element_type=f32) + lax.dot_general(
        rows[:, width:].astype(f32), qk_ref[...], NT, precision=highest, preferred_element_type=f32
    )
    channels = patch_ref.shape[0]
    for c in range(PIX):
        patch_ref[:, c, :] = total[c * channels : (c + 1) * channels]
    table_ref[...] = total[own_rows : own_rows + table_ref.shape[0]]


def finish_tail(member, tails, stacked, pick, agg_value, query_keys, agg_key, agg_query, channels, lines):
    groups = len(tails)
    width = agg_value.shape[0]
    own = width // groups
    args = [*tails, stacked, pick, agg_value, query_keys]
    spec = pltpu.PrefetchScalarGridSpec(
        num_scalar_prefetch=1,
        grid=(1,),
        in_specs=whole_blocks([x.shape for x in args])
        + [pl.BlockSpec((width, own), lambda i, m: (0, m[0])), pl.BlockSpec((1, width), lambda i, m: (0, 0))],
        out_specs=whole_blocks([(own, width), (own, width), (1, own), (channels, PIX, width), (lines, width)]),
        scratch_shapes=[pltpu.VMEM((width, query_keys.shape[1]), f32)],
    )
    return pl.pallas_call(
        partial(tail_kernel, groups=groups),
        grid_spec=spec,
        out_shape=[
            jax.ShapeDtypeStruct((own, width), f32),
            jax.ShapeDtypeStruct((own, width), f32),
            jax.ShapeDtypeStruct((1, own), f32),
            jax.ShapeDtypeStruct((channels, PIX, width), f32),
            jax.ShapeDtypeStruct((lines, width), f32),
        ],
        cost_estimate=LIGHT,
        name="finish_tail",
    )(member, *args, agg_key, agg_query)


def fence(*values):
    return lax.optimization_barrier(values)


def swap(value, axis, bits):
    size = lax.axis_size(axis)
    return lax.ppermute(value, axis, [(i, i ^ bits) for i in range(size)])


def from_all(own, groups):
    return [own] + [swap(own, "var", k) for k in range(1, groups)]


def exchange(value):
    return lax.all_to_all(value, "var", split_axis=0, concat_axis=0, tiled=True)


def chip_bits():
    bits, bit = [], 1
    while bit < lax.axis_size("chip"):
        bits.append(bit)
        bit *= 2
    return bits


def mirrored(levels):
    return levels == 2


def partner(bit):
    levels = len(chip_bits())
    return 3 if mirrored(levels) and bit == 2 else bit


def low_bit(chip, levels):
    return (chip ^ (chip >> 1)) & 1 if mirrored(levels) else chip & 1


def is_high(bit):
    chip = lax.axis_index("chip")
    return low_bit(chip, len(chip_bits())) if bit == 1 else (chip // bit) % 2


def stack_other(value, bit):
    return jnp.concatenate([value, swap(value, "chip", partner(bit))], axis=0)


def with_core(halves):
    return [*halves, *(swap(value, "core", 1) for value in halves)]


def by_core(mine, other, core):
    return jnp.where(core == 0, mine, other), jnp.where(core == 0, other, mine)


def body(
    field_patches,
    var_ids,
    lead_bucket,
    patch_weight,
    var_embed,
    agg_query,
    agg_key,
    agg_value,
    agg_out,
    lead_table,
    ln1_gain,
    attn_qkv,
    attn_out,
    ln2_gain,
    mlp_in,
    mlp_in_bias,
    mlp_out,
    cotangent,
):
    groups = lax.axis_size("var")
    member = lax.axis_index("var")
    core = lax.axis_index("core")
    channels, pixel_count, samples, seq = field_patches.shape
    width = agg_key.shape[0]
    inner_width = mlp_in.shape[1]
    leads = lead_table.shape[0]
    vocab = var_embed.shape[0]
    rows = seq // groups
    own = width // groups
    count = channels * groups
    slots = [member ^ k for k in range(groups)]
    member_one = member.reshape(1).astype(jnp.int32)
    core_one = core.reshape(1).astype(jnp.int32)
    bits = chip_bits()
    assert bits
    high = is_high(bits[0])
    high_one = high.reshape(1).astype(jnp.int32)
    half = width // 2
    gain_one = ln1_gain.astype(f32)
    gain_two = ln2_gain.astype(f32)

    mine = jnp.concatenate(
        [
            field_patches.reshape(channels, pixel_count, seq),
            patch_weight,
        ],
        axis=2,
    )
    grad_out = cotangent.reshape(rows, width)
    grad_act = lax.dot_general(grad_out, mlp_out, NT, preferred_element_type=f32).astype(bf16)
    ids = jnp.concatenate([lax.dynamic_slice_in_dim(var_ids, slot * channels, channels) for slot in slots])
    table_pick = (ids[:, None] == jnp.arange(vocab, dtype=jnp.int32)[None, :]).astype(bf16)
    head_of = jnp.arange(width, dtype=jnp.int32) // HEAD_DIM
    spread = head_of[:, None] == jnp.arange(2 * HEAD_DIM, dtype=jnp.int32)[None, :]
    query_block = jnp.where(spread, agg_query[:, None], jnp.zeros((), bf16))
    query_keys = jnp.dot(agg_key, query_block, preferred_element_type=f32) * 0.125
    grad_out_other = swap(lax.dynamic_slice_in_dim(grad_out, (1 - core) * half, half, axis=1), "core", 1)
    arrived, grad_act, table_pick, query_keys, grad_out_other = fence(
        from_all(mine, groups), grad_act, table_pick, query_keys, grad_out_other
    )
    pixels, key_rows, values, values_t, by_slot = prepare(
        arrived, table_pick, var_embed, query_keys, agg_value, seq
    )

    hidden_t, qkv, resid_zero, att_low = front(
        member_one, lead_bucket, pixels, key_rows, values_t, agg_out, lead_table, gain_one[None], attn_qkv, groups
    )

    hidden_t, att_low, qkv = fence(hidden_t, att_low, qkv)
    hidden_other, att_other = swap(hidden_t, "core", 1), swap(att_low, "core", 1)

    block = min(512, rows)
    mixed_parts, lse_parts, received = [None] * groups, [None] * groups, [None] * groups
    for k in reversed(range(groups)):
        mixed_parts[k], lse_parts[k] = attend(member_one, qkv, k, rows, block)
        if k + 1 < groups:
            received[k + 1], mixed_parts[k], qkv = fence(received[k + 1], mixed_parts[k], qkv)
            if k + 2 == groups:
                hidden_other, att_other, qkv = fence(hidden_other, att_other, qkv)
        received[k] = swap(mixed_parts[k], "var", k) if k else mixed_parts[k]

    act, act_t, gu_send, gu_keep, grad_bias, resid_one, hidden_two_t, mixed_t = inner_part(
        member_one, core_one, received, attn_out, resid_zero, gain_two[None], mlp_in, mlp_in_bias.astype(f32)[None], grad_act
    )
    gu_send, act_t, act, hidden_two_t, mixed_t = fence(gu_send, act_t, act, hidden_two_t, mixed_t)
    act_other, gu_other, hidden_two_other, mixed_other = (
        swap(value, "core", 1) for value in (act_t, gu_send, hidden_two_t, mixed_t)
    )
    output, grad_resid_one, grad_branch, branch_send, grad_mixed, grad_gain_two = outer_part(
        core_one, act, gu_send, gu_keep, mlp_in, mlp_out, attn_out, resid_one, gain_two[None], grad_out, groups
    )
    act_other, gu_other, hidden_two_other, mixed_other, grad_mixed, branch_send, output = fence(
        act_other, gu_other, hidden_two_other, mixed_other, grad_mixed, branch_send, output
    )
    output = output.reshape(samples, rows, width)

    branch_other = swap(branch_send, "core", 1)
    grad_heads = exchange(grad_mixed).reshape(seq, own)
    branch_other, act_t, act_other = fence(branch_other, act_t, act_other)
    out_y, out_y_send, out_x, out_x_send = out_grad(core_one, act_t, act_other, grad_out, grad_out_other)
    branch_other, out_y, out_y_send, out_x, out_x_send = fence(branch_other, out_y, out_y_send, out_x, out_x_send)
    in_part, in_part_send = in_grad(
        core_one,
        high_one,
        hidden_two_t,
        hidden_two_other,
        gu_keep,
        gu_other,
        mixed_t,
        mixed_other,
        grad_branch,
        branch_other,
    )
    out_y_came, out_x_came = swap(out_y_send, "var", 2), swap(out_x_send, "var", 1)
    grad_heads, in_part_send, in_part = fence(grad_heads, in_part_send, in_part)

    pair = 2 * HEAD_DIM
    pairs = own // pair
    assert pairs == 2
    in_part_came = swap(in_part_send, "chip", bits[0])
    first = attend_back(member_one, qkv, grad_heads, mixed_parts, lse_parts, 0, 512)
    first, qkv, out_y_came, out_x_came = fence(first, qkv, out_y_came, out_x_came)
    out_y, out_y_send = split_add(out_y, out_y_came, 2)
    out_x, out_x_send = split_add(out_x, out_x_came, 2)
    first, qkv, out_y_send, out_x_send = fence(first, qkv, out_y_send, out_x_send)
    first_came = exchange(first)
    first_other = swap(first, "core", 1)
    out_y_came, out_x_came = swap(out_y_send, "var", 1), swap(out_x_send, "var", 2)
    second = attend_back(member_one, qkv, grad_heads, mixed_parts, lse_parts, 1, 512)
    second_came = exchange(second)
    first_came, first_other, second, in_part_came, out_y_came, out_x_came = fence(
        first_came, first_other, second, in_part_came, out_y_came, out_x_came
    )
    second_other = swap(second, "core", 1)
    out_keep, out_send = choose(high_one, out_y, out_y_came, out_x, out_x_came)
    out_came = swap(out_send, "chip", bits[0])
    in_y, in_y_send, in_x, in_x_send = split_add(in_part, in_part_came, 4)
    second_other, in_y_send, in_x_send = fence(second_other, in_y_send, in_x_send)
    weight_qkv = qkv_grad(core_one, hidden_t, hidden_other, (first, second), (first_other, second_other))
    second_came, weight_qkv, in_y_send, in_x_send, grad_resid_one, out_came = fence(
        second_came, weight_qkv, in_y_send, in_x_send, grad_resid_one, out_came
    )
    rest = bits[1:]

    def scatter_parts(keep, came, bit):
        return [pick_add(keep, came, which, 0) for which in (is_high(bit), 1 - is_high(bit))]

    def scatter_step(keep, came, bit):
        keep, send = scatter_parts(keep, came, bit)
        return keep, swap(send, "chip", partner(bit))

    out_keep, out_send = scatter_parts(out_keep, out_came, rest[0])
    second_came, out_send, in_y_send, in_x_send = fence(second_came, out_send, in_y_send, in_x_send)
    out_came = swap(out_send, "chip", partner(rest[0]))
    in_y_came, in_x_came = swap(in_y_send, "var", 2), swap(in_x_send, "var", 1)
    grad_agg, grad_agg_send, grad_att, grad_gain_one, sample_sum = join(
        core_one, first_came, second_came, attn_qkv, resid_zero, gain_one[None], grad_resid_one, agg_out
    )
    grad_agg, grad_agg_send, grad_att, out_came, in_y_came, in_x_came = fence(
        grad_agg, grad_agg_send, grad_att, out_came, in_y_came, in_x_came
    )
    for bit in rest[1:]:
        out_keep, out_came = scatter_step(out_keep, out_came, bit)
    out_rows = add(out_keep, out_came)
    in_y, in_y_send = split_add(in_y, in_y_came, 2)
    in_x, in_x_send = split_add(in_x, in_x_came, 2)
    out_rows, grad_att, grad_agg_send, in_y_send, in_x_send = fence(
        out_rows, grad_att, grad_agg_send, in_y_send, in_x_send
    )
    out_other = swap(out_rows, "chip", partner(rest[-1]))
    grad_agg_other = swap(grad_agg_send, "core", 1)
    in_y_came, in_x_came = swap(in_y_send, "var", 1), swap(in_x_send, "var", 2)

    field_own, tail, tail_send = aggregate_back(
        member_one,
        core_one,
        lead_bucket,
        pixels,
        key_rows,
        values,
        grad_att,
        (grad_bias, grad_gain_two, grad_gain_one, sample_sum),
        groups,
    )
    tail, tail_send, grad_agg_other, in_y_came, in_x_came = fence(
        tail, tail_send, grad_agg_other, in_y_came, in_x_came
    )
    tail_came = swap(tail_send, "core", 1)
    in_own = jnp.concatenate([add(in_y, in_y_came), add(in_x, in_x_came)], axis=0)
    for bit in rest:
        in_rows = in_own.shape[0] // 2
        in_own, in_send = (
            lax.dynamic_slice_in_dim(in_own, which * in_rows, in_rows) for which in (is_high(bit), 1 - is_high(bit))
        )
        if bit != rest[-1]:
            in_own = add(in_own, swap(in_send, "chip", partner(bit)))
    in_send, grad_agg_other, tail_came = fence(in_send, grad_agg_other, tail_came)
    in_came = swap(in_send, "chip", partner(rest[-1]))
    tail = add(tail, tail_came)
    deep = tail.shape[0] // 2
    tail, grad_agg_other = fence(tail, grad_agg_other)
    tail_came = swap(tail[deep:], "var", 1)
    last_send = last_grad(core_one, weight_qkv, att_low, att_other, grad_agg, grad_agg_other, groups)
    tail, tail_came, last_send, out_other = fence(tail, tail_came, last_send, out_other)
    tail = add(tail[:deep], tail_came)
    deep //= 2
    tail_came = swap(tail[deep:], "var", 2)
    out_rows = jnp.concatenate([out_rows, out_other], axis=0)
    for bit in reversed(rest[:-1]):
        out_rows = stack_other(out_rows, bit)
    tail, tail_came, last_send, out_rows, in_came = fence(tail, tail_came, last_send, out_rows, in_came)
    last_came = exchange(last_send)
    in_rows = add(in_own, in_came)
    tail = add(tail[:deep], tail_came)
    in_rows, tail, out_rows = fence(in_rows, tail, out_rows)
    in_other = swap(in_rows, "chip", partner(rest[-1]))
    tail_came = swap(tail, "chip", bits[0])
    out_other = swap(out_rows, "chip", bits[0])
    last_came, tail, out_rows = fence(last_came, tail, out_rows)
    last_keep, last_send = gather_sources(high_one, last_came, 3 * pair)
    last_send, tail, tail_came, in_other = fence(last_send, tail, tail_came, in_other)
    last_came = swap(last_send, "chip", bits[0])
    tail = add(tail, tail_came)
    for bit in rest:
        tail_came = swap(tail, "chip", partner(bit))
        if bit != rest[-1]:
            tail = add(tail, tail_came)
    tail, tail_came, out_rows, out_other = fence(tail, tail_came, out_rows, out_other)
    tail = add(tail, tail_came)
    tail_came = swap(tail, "core", 1)
    out_pieces = with_core([out_rows, out_other])
    tail, tail_came, out_pieces = fence(tail, tail_came, out_pieces)
    levels = len(bits)
    where = jnp.stack([lax.axis_index("chip"), core]).astype(jnp.int32)
    (sum_mlp_out,) = assemble(where, out_pieces, levels, [(0, 0, half, 0, half, 0)], [width])
    low, up = by_core(tail, tail_came, core)
    tail = jnp.concatenate([low[:, :half], up], axis=1)
    tail, sum_mlp_out, last_came, in_other = fence(tail, sum_mlp_out, last_came, in_other)
    for bit in rest[:-1]:
        last_keep, last_came = scatter_step(last_keep, last_came, bit)
    last_keep, last_send = scatter_parts(last_keep, last_came, rest[-1])
    in_rows = jnp.concatenate([in_rows, in_other], axis=0)
    for bit in reversed(rest[:-1]):
        in_rows = stack_other(in_rows, bit)
    tail, last_send, in_rows = fence(tail, last_send, in_rows)
    last_came = swap(last_send, "chip", partner(rest[-1]))
    tails = from_all(tail, groups)
    in_other = swap(in_rows, "chip", bits[0])
    tails = fence(*tails)
    stride = tail.shape[0]
    per_slot = (PIX + 1) * channels
    small_sum = tail[per_slot:, :width].astype(f32)
    part_size = inner_width // groups
    sum_bias = small_sum[0]
    sum_gain_two = small_sum[1, :own]
    sum_gain_one = small_sum[1, own : 2 * own]
    sum_lead = small_sum[2 : 2 + leads // groups]

    own_ids = member * (vocab // groups) + jnp.arange(16, dtype=jnp.int32)
    own_pick = jnp.where(jnp.arange(16)[:, None] < vocab // groups, own_ids[:, None] == ids[None, :], False)
    own_pick = jnp.pad(
        own_pick.reshape(16, groups, channels), ((0, 0), (0, 0), (PIX * channels, stride - per_slot))
    ).reshape(16, groups * stride)
    sum_value, sum_key, sum_query, sum_patch, sum_table = finish_tail(
        member_one,
        tails,
        by_slot,
        own_pick.astype(bf16),
        agg_value,
        query_keys,
        agg_key,
        agg_query.astype(f32)[None],
        channels,
        vocab // groups,
    )
    sum_query = sum_query.reshape(own)
    sum_value, last_came, in_rows = fence(sum_value, last_came, in_rows)
    last_rows = add(last_keep, last_came)
    last_other = swap(last_rows, "chip", partner(rest[-1]))
    field_slots = field_own.reshape(pixel_count, groups, channels, rows)
    field_parts = [swap(field_slots[:, k], "var", k) if k else field_slots[:, 0] for k in range(groups)]
    field_parts = fence(*field_parts)
    field_grad = place_field(member_one, field_parts).reshape(channels, pixel_count, samples, seq)
    field_grad, last_other, in_rows, in_other = fence(field_grad, last_other, in_rows, in_other)
    last_rows = jnp.concatenate([last_rows, last_other], axis=0)
    for bit in reversed(rest[:-1]):
        last_rows = stack_other(last_rows, bit)
    last_rows, in_rows, in_other = fence(last_rows, in_rows, in_other)
    last_other = swap(last_rows, "chip", bits[0])
    in_pieces = fence(*with_core([in_rows, in_other]))

    half_in = inner_width // 2
    units = half_in // 2
    sum_mlp_in, sum_attn_out = assemble(
        where,
        in_pieces,
        levels,
        [(0, 0, units, 0, half_in, units), (1, units, half // 2, 0, half, half // 2)],
        [inner_width, width],
        low_rows=False,
    )
    sum_mlp_in, last_rows, last_other, sum_patch, sum_table, field_grad = fence(
        sum_mlp_in, last_rows, last_other, sum_patch, sum_table, field_grad
    )
    sum_qkv, sum_agg_out = assemble(
        where,
        with_core([last_rows, last_other]),
        levels,
        [
            (0, (3 * p + t) * pair, pair, t * width + p * own, pair, 0)
            for p in range(groups)
            for t in range(3)
        ]
        + [(1, groups * 3 * pair, half, 0, half, 0)],
        [3 * width, width],
    )
    return (
        output,
        field_grad,
        sum_patch,
        sum_table,
        sum_query,
        sum_key,
        sum_value,
        sum_agg_out,
        sum_lead,
        sum_gain_one,
        sum_qkv,
        sum_attn_out,
        sum_gain_two,
        sum_mlp_in,
        sum_bias,
        sum_mlp_out,
    )


def solution(mesh):
    members, patches = mesh.shape["var"], mesh.shape["patch"]
    chips = Mesh(mesh.devices.reshape(members, patches // 2, 2), ("var", "chip", "core"))
    patch = ("chip", "core")
    placed = (
        P("var", None, patch, None),
        P(),
        P(patch),
        P("var", None, None),
        *[P()] * 13,
        P(patch, "var", None),
    )
    return jax.shard_map(
        body,
        mesh=chips,
        in_specs=placed,
        out_specs=(
            P(patch, "var", None),
            P("var", None, patch, None),
            P("var", None, None),
            P("var", None),
            P("var"),
            P("var", None),
            P("var", None),
            P("var", None),
            P("var", None),
            P("var"),
            P("var", None),
            P("var", None),
            P("var"),
            P("var", None),
            P("var"),
            P("var", None),
        ),
        check_vma=False,
    )
```

profile of v0, /device:TPU:0, one launch (start us, length us, event | category | flops | bytes accessed | tf_op | source)
XLA Modules:
  0.0 415.7 jit_solution(15137106062647819466)
XLA Ops:
  1.8 3.0 collective-permute-start
  7.5 10.4 %convolution_convert_fusion.ga_ref = bf16[512,4096]{1,0:T(8,128)(2,1)} fusion(bf16[4096,1024]{1,0:T(8,128)(2,1)} %w2_ref.1, bf16[1,512,1024]{2,1,0:T(8,128)(2,1)} %param.35), kind=kOutput, calls=%fused_computation | convolution fusion | flops 4297064448 | bytes 13631488 | tf_op jit(solution)/shard_map/dot_general | solution.py:1146
  21.8 6.1 %prepare.1 = (f32[4,48,2048]{2,1,0:T(8,128)}, f32[5,48,128]{2,1,0:T(8,128)}, bf16[240,1024]{1,0:T(8,128)(2,1)}, bf16[1024,240]{1,0:T(8,128)(2,1)}, bf16[256,1024]{1,0:T(8,128)(2,1)}) custom-call(bf16[12,4,3072]{2,1,0:T(4,128)(2,1)} %copy-done.13, bf16[12,4,3072]{2,1,0:T(4,128)(2,1)} %collective-permute-done.refs_1_, ...), custom_call_target="tpu_custom_call" | custom-call | flops 1 | bytes 1 | tf_op jit(solution)/shard_map/prepare/pallas_call | solution.py:79
  27.8 23.4 %front.1 = (bf16[1024,2048]{1,0:T(8,128)(2,1)}, bf16[2048,768]{1,0:T(8,128)(2,1)}, f32[512,1024]{1,0:T(8,128)}, bf16[1024,512]{1,0:T(8,128)(2,1)}) custom-call(s32[1]{0:T(128)} %bitcast.member, s32[1]{0:T(128)S(6)} %copy.56.bucket, f32[4,48,2048]{2,1,0:T(8,128)} %get-tuple-element.238.pixel_ref, f32[5,48,128]{2,1,0:T(8,128)} %get-tuple-element.239.key_ref, ...), custom_call_target="tpu_custom_call" | custom-call | flops 1 | bytes 1 | tf_op jit(solution)/shard_map/front/pallas_call | solution.py:166
  51.9 7.8 %attend.4 = (bf16[512,256]{1,0:T(8,128)(2,1)}, f32[2,2,512]{2,1,0:T(2,128)}) custom-call(s32[1]{0:T(128)} %bitcast.member, bf16[2048,768]{1,0:T(8,128)(2,1)} %get-tuple-element.312.q_ref.k_ref.v_ref, bf16[2048,768]{1,0:T(8,128)(2,1)} %get-tuple-element.312.q_ref.k_ref.v_ref, bf16[2048,768]{1,0:T(8,128)(2,1)} %get-tuple-element.312.q_ref.k_ref.v_ref), custom_call_target="tpu_custom_call" | custom-call | flops 1 | bytes 1 | tf_op jit(solution)/shard_map/attend/pallas_call | solution.py:228
  59.7 2.9 collective-permute-start.4
  62.7 7.8 %attend.5 = (bf16[512,256]{1,0:T(8,128)(2,1)}, f32[2,2,512]{2,1,0:T(2,128)}) custom-call(s32[1]{0:T(128)} %bitcast.member, bf16[2048,768]{1,0:T(8,128)(2,1)} %get-tuple-element.312.q_ref.k_ref.v_ref, bf16[2048,768]{1,0:T(8,128)(2,1)} %get-tuple-element.312.q_ref.k_ref.v_ref, bf16[2048,768]{1,0:T(8,128)(2,1)} %get-tuple-element.312.q_ref.k_ref.v_ref), custom_call_target="tpu_custom_call" | custom-call | flops 1 | bytes 1 | tf_op jit(solution)/shard_map/attend/pallas_call | solution.py:228
  71.5 8.2 %attend.6 = (bf16[512,256]{1,0:T(8,128)(2,1)}, f32[2,2,512]{2,1,0:T(2,128)}) custom-call(s32[1]{0:T(128)} %bitcast.member, bf16[2048,768]{1,0:T(8,128)(2,1)} %get-tuple-element.312.q_ref.k_ref.v_ref, bf16[2048,768]{1,0:T(8,128)(2,1)} %get-tuple-element.312.q_ref.k_ref.v_ref, bf16[2048,768]{1,0:T(8,128)(2,1)} %get-tuple-element.312.q_ref.k_ref.v_ref), custom_call_target="tpu_custom_call" | custom-call | flops 1 | bytes 1 | tf_op jit(solution)/shard_map/attend/pallas_call | solution.py:228
  82.5 7.8 %attend.7 = (bf16[512,256]{1,0:T(8,128)(2,1)}, f32[2,2,512]{2,1,0:T(2,128)}) custom-call(s32[1]{0:T(128)} %bitcast.member, bf16[2048,768]{1,0:T(8,128)(2,1)} %get-tuple-element.312.q_ref.k_ref.v_ref, bf16[2048,768]{1,0:T(8,128)(2,1)} %get-tuple-element.312.q_ref.k_ref.v_ref, bf16[2048,768]{1,0:T(8,128)(2,1)} %get-tuple-element.312.q_ref.k_ref.v_ref), custom_call_target="tpu_custom_call" | custom-call | flops 1 | bytes 1 | tf_op jit(solution)/shard_map/attend/pallas_call | solution.py:228
  91.0 21.1 %inner_part.1 = (bf16[512,4096]{1,0:T(8,128)(2,1)}, bf16[4096,512]{1,0:T(8,128)(2,1)}, bf16[512,2048]{1,0:T(8,128)(2,1)}, bf16[512,2048]{1,0:T(8,128)(2,1)}, f32...) custom-call(s32[1]{0:T(128)} %bitcast.member, s32[1]{0:T(128)} %bitcast.1.core, ...), custom_call_target="tpu_custom_call" | custom-call | flops 1 | bytes 1 | tf_op jit(solution)/shard_map/inner_part/pallas_call | solution.py:507
  113.3 20.9 %outer_part.1 = (bf16[512,1024]{1,0:T(8,128)(2,1)}, f32[512,1024]{1,0:T(8,128)}, bf16[512,1024]{1,0:T(8,128)(2,1)}, bf16[512,512]{1,0:T(8,128)(2,1)}, bf16[4,512,256]{2,1,0:T(8,128)(2,1)}, /*index=5*/f32[1,1024]{1,0:T(1,128)}) custom-call(s32[1]{0:T(128)} %bitcast.1.core, bf16[512,4096]{1,0:T(8,128)(2,1)} %get-tuple-element.271.act_ref, ...), custom_call_target="tpu_custom_call" | custom-call | flops 1 | bytes 1 | tf_op jit(solution)/shard_map/outer_part/pallas_call | solution.py:593
  135.2 4.0 all-to-all-start
  139.2 9.6 %out_grad.1 = (bf16[1024,512]{1,0:T(8,128)(2,1)}, bf16[1024,512]{1,0:T(8,128)(2,1)}, bf16[1024,512]{1,0:T(8,128)(2,1)}, bf16[1024,512]{1,0:T(8,128)(2,1)}) custom-call(s32[1]{0:T(128)} %bitcast.1.core, bf16[4096,512]{1,0:T(8,128)(2,1)} %get-tuple-element.282.left, bf16[4096,512]{1,0:T(8,128)(2,1)} %collective-permute-done.9.left_other, ...), custom_call_target="tpu_custom_call" | custom-call | flops 1 | bytes 1 | tf_op jit(solution)/shard_map/out_grad/pallas_call | solution.py:639
  152.2 11.5 %in_grad.1 = (bf16[1024,1280]{1,0:T(8,128)(2,1)}, bf16[1024,1280]{1,0:T(8,128)(2,1)}) custom-call(s32[1]{0:T(128)} %bitcast.1.core, s32[1]{0:T(128)} %bitcast.11.high, bf16[1024,512]{1,0:T(8,128)(2,1)} %get-tuple-element.269.h, bf16[1024,512]{1,0:T(8,128)(2,1)} %copy-done.15, bf16[512,2048]{1,0:T(8,128)(2,1)} %get-tuple-element.272.keep_ref.u, ...), custom_call_target="tpu_custom_call" | custom-call | flops 1 | bytes 1 | tf_op jit(solution)/shard_map/in_grad/pallas_call | solution.py:692
  165.4 24.6 %attend_back.2.refs_0_ = bf16[2048,384]{1,0:T(8,128)(2,1)} custom-call(s32[1]{0:T(128)} %bitcast.member, bf16[2048,768]{1,0:T(8,128)(2,1)} %get-tuple-element.312.q_ref.k_ref.v_ref, bf16[2048,768]{1,0:T(8,128)(2,1)} %get-tuple-element.312.q_ref.k_ref.v_ref, bf16[2048,768]{1,0:T(8,128)(2,1)} %get-tuple-element.312.q_ref.k_ref.v_ref, ...), custom_call_target="tpu_custom_call" | custom-call | flops 1 | bytes 1 | tf_op jit(solution)/shard_map/attend_back/pallas_call | solution.py:310
  190.1 3.2 add_convert_fusion.4
  193.3 3.7 all-to-all-start.1
  197.0 2.1 collective-permute-start.18
  200.6 24.6 %attend_back.3.refs_1_ = bf16[2048,384]{1,0:T(8,128)(2,1)} custom-call(s32[1]{0:T(128)} %bitcast.member, bf16[2048,768]{1,0:T(8,128)(2,1)} %get-tuple-element.312.q_ref.k_ref.v_ref, bf16[2048,768]{1,0:T(8,128)(2,1)} %get-tuple-element.312.q_ref.k_ref.v_ref, bf16[2048,768]{1,0:T(8,128)(2,1)} %get-tuple-element.312.q_ref.k_ref.v_ref, ...), custom_call_target="tpu_custom_call" | custom-call | flops 1 | bytes 1 | tf_op jit(solution)/shard_map/attend_back/pallas_call | solution.py:310
  225.1 3.4 collective-permute-done.18.b
  229.8 3.6 all-to-all-start.2
  233.4 2.4 choose.1
  236.7 4.2 %add_convert_fusion = (bf16[256,1280]{1,0:T(8,128)(2,1)S(1)}, bf16[256,1280]{1,0:T(8,128)(2,1)S(1)}, bf16[256,1280]{1,0:T(8,128)(2,1)}, bf16[256,1280]{1,0:T(8,128)(2,1)}) fusion(bf16[1024,1280]{1,0:T(8,128)(2,1)} %collective-permute-done.17, bf16[1024,1280]{1,0:T(8,128)(2,1)} %get-tuple-element.322), kind=kLoop, calls=%fused_computation.1 | loop fusion | flops 5242880 | bytes 7864320 | tf_op jit(solution)/shard_map/convert_element_type | solution.py:844
  240.9 9.7 %qkv_grad.1.qkv_ref = bf16[1024,384]{1,0:T(8,128)(2,1)} custom-call(s32[1]{0:T(128)} %bitcast.1.core, bf16[1024,2048]{1,0:T(8,128)(2,1)} %get-tuple-element.248.h, bf16[1024,2048]{1,0:T(8,128)(2,1)} %collective-permute-done.6.h_other, bf16[2048,384]{1,0:T(8,128)(2,1)} %attend_back.2.refs_0_, bf16[2048,384]{1,0:T(8,128)(2,1)} %attend_back.3.refs_1_, ...), custom_call_target="tpu_custom_call" | custom-call | flops 1 | bytes 1 | tf_op jit(solution)/shard_map/qkv_grad/pallas_call | solution.py:721
  250.6 2.1 all-to-all-done.2
  256.2 2.9 collective-permute-start.22
  259.1 13.7 %join.1 = (bf16[512,1024]{1,0:T(8,128)(2,1)}, bf16[512,512]{1,0:T(8,128)(2,1)}, bf16[1024,512]{1,0:T(8,128)(2,1)}, f32[1,1024]{1,0:T(1,128)}, f32[1,1024]{1,0:T(1,128)}) custom-call(s32[1]{0:T(128)} %bitcast.1.core, bf16[2048,384]{1,0:T(8,128)(2,1)} %bitcast.47, bf16[2048,384]{1,0:T(8,128)(2,1)} %bitcast.48, bf16[1024,3072]{1,0:T(8,128)(2,1)} %wv.1, ...), custom_call_target="tpu_custom_call" | custom-call | flops 1 | bytes 1 | tf_op jit(solution)/shard_map/join/pallas_call | solution.py:828
  279.5 6.6 %aggregate_back.1 = (bf16[4,48,512]{2,1,0:T(8,128)(2,1)}, bf16[256,640]{1,0:T(8,128)(2,1)}, bf16[256,640]{1,0:T(8,128)(2,1)}) custom-call(s32[1]{0:T(128)} %bitcast.member, s32[1]{0:T(128)} %bitcast.1.core, s32[1]{0:T(128)S(6)} %copy.56.bucket, f32[4,48,2048]{2,1,0:T(8,128)} %get-tuple-element.238.pixel_ref, f32[5,48,128]{2,1,0:T(8,128)} %get-tuple-element.239.key_ref, ...), custom_call_target="tpu_custom_call" | custom-call | flops 1 | bytes 1 | tf_op jit(solution)/shard_map/aggregate_back/pallas_call | solution.py:408
  291.5 2.2 collective-permute-start.32
  293.7 5.1 %last_grad.1 = bf16[4,256,896]{2,1,0:T(8,128)(2,1)} custom-call(s32[1]{0:T(128)} %bitcast.1.core, bf16[1024,384]{1,0:T(8,128)(2,1)} %qkv_grad.1.qkv_ref, bf16[1024,512]{1,0:T(8,128)(2,1)} %get-tuple-element.249.a, bf16[1024,512]{1,0:T(8,128)(2,1)} %copy-done.14, bf16[512,1024]{1,0:T(8,128)(2,1)} %get-tuple-element.367.g, bf16[512,512]{1,0:T(8,128)(2,1)} %copy-done.22), custom_call_target="tpu_custom_call" | custom-call | flops 1 | bytes 1 | tf_op jit(solution)/shard_map/last_grad/pallas_call | solution.py:753
  300.4 2.9 collective-permute-done.31
  304.1 3.8 all-to-all-start.3
  310.9 4.5 %collective-permute-start.36 = (bf16[512,512]{1,0:T(8,128)(2,1)S(1)}, bf16[512,512]{1,0:T(8,128)(2,1)S(1)}, u32[]{:S(2)}, u32[]{:S(2)}) collective-permute-start(bf16[512,512]{1,0:T(8,128)(2,1)S(1)} %pad_maximum_fusion.1.refs_0_), channel_id=1, source_target_pairs={{0,2},{2,0},{4,6},{6,4},{1,3},{3,1},{5,7},{7,5},{8,10},{10,8},{12,... | collective-permute-start | bytes 1572872 | tf_op jit(solution)/shard_map/ppermute | solution.py:1047
  315.4 13.7 %all-to-all-done.3.came_ref = bf16[4,256,896]{2,1,0:T(8,128)(2,1)S(1)} async-done(((bf16[4,256,896]{2,1,0:T(8,128)(2,1)}), bf16[4,256,896]{2,1,0:T(8,128)(2,1)S(1)}, u32[]{:S(2)}, u32[]{:S(2)}) %all-to-all-start.3) | async-done | bytes 1835040 | tf_op jit(solution)/shard_map/all_to_all | solution.py:1055
  330.3 2.6 gather_sources.1
  332.9 2.0 collective-permute-start.35
  335.0 4.2 %collective-permute-done.35 = bf16[64,640]{1,0:T(8,128)(2,1)S(1)} collective-permute-done((bf16[64,640]{1,0:T(8,128)(2,1)S(1)}, bf16[64,640]{1,0:T(8,128)(2,1)S(1)}, u32[]{:S(2)}, u32[]{:S(2)}) %collective-permute-start.35) | collective-permute-done | bytes 81952 | tf_op jit(solution)/shard_map/ppermute | solution.py:1047
  340.5 3.4 collective-permute-start.40
  344.8 4.6 %assemble.3 = f32[1024,1024]{1,0:T(8,128)} custom-call(s32[2]{0:T(128)} %pad_add_fusion.1.where, bf16[512,512]{1,0:T(8,128)(2,1)} %copy-done.8, bf16[512,512]{1,0:T(8,128)(2,1)} %copy-done.23, bf16[512,512]{1,0:T(8,128)(2,1)} %copy-done.24, bf16[512,512]{1,0:T(8,128)(2,1)} %copy-done.25), custom_call_target="tpu_custom_call" | custom-call | flops 1 | bytes 1 | tf_op jit(solution)/shard_map/assemble/pallas_call | solution.py:948
  349.5 7.2 %collective-permute-done.40 = bf16[128,2048]{1,0:T(8,128)(2,1)S(1)} collective-permute-done((bf16[128,2048]{1,0:T(8,128)(2,1)}, bf16[128,2048]{1,0:T(8,128)(2,1)S(1)}, u32[]{:S(2)}, u32[]{:S(2)}) %collective-permute-start.40) | collective-permute-done | bytes 524320 | tf_op jit(solution)/shard_map/ppermute | solution.py:1047
  361.5 2.2 collective-permute-start.44
  368.1 6.2 %finish_tail.1 = (f32[256,1024]{1,0:T(8,128)}, f32[256,1024]{1,0:T(8,128)}, f32[1,256]{1,0:T(1,128)}, f32[12,4,1024]{2,1,0:T(4,128)}, f32[12,1024]{1,0:T(8,128)}) custom-call(s32[1]{0:T(128)} %bitcast.member, bf16[64,1152]{1,0:T(8,128)(2,1)} %copy-done.20, bf16[64,1152]{1,0:T(8,128)(2,1)} %copy-done.37, bf16[64,1152]{1,0:T(8,128)(2,1)} %collective-permute-done.42.refs_2_, ...), custom_call_target="tpu_custom_call" | custom-call | flops 1 | bytes 1 | tf_op jit(solution)/shard_map/finish_tail/pallas_call | solution.py:1026
  375.4 2.2 collective-permute-start.48
  383.2 2.0 collective-permute-done.47.refs_3_
  387.6 2.8 collective-permute-done.48
  393.7 5.0 %assemble.4 = (f32[256,4096]{1,0:T(8,128)}, f32[256,1024]{1,0:T(8,128)}) custom-call(s32[2]{0:T(128)} %pad_add_fusion.1.where, bf16[256,1280]{1,0:T(8,128)(2,1)} %copy-done.4, bf16[256,1280]{1,0:T(8,128)(2,1)} %copy-done.18, bf16[256,1280]{1,0:T(8,128)(2,1)} %copy-done.19, bf16[256,1280]{1,0:T(8,128)(2,1)} %collective-permute-done.51.refs_3_), custom_call_target="tpu_custom_call" | custom-call | flops 1 | bytes 1 | tf_op jit(solution)/shard_map/assemble/pallas_call | solution.py:948
  398.7 6.3 %collective-permute-done.52.refs_1_ = bf16[128,2048]{1,0:T(8,128)(2,1)} collective-permute-done((bf16[128,2048]{1,0:T(8,128)(2,1)S(1)}, bf16[128,2048]{1,0:T(8,128)(2,1)}, u32[]{:S(2)}, u32[]{:S(2)}) %collective-permute-start.52) | collective-permute-done | bytes 524320 | tf_op jit(solution)/shard_map/ppermute | solution.py:1047
  410.8 4.7 %assemble.5 = (f32[256,3072]{1,0:T(8,128)}, f32[256,1024]{1,0:T(8,128)}) custom-call(s32[2]{0:T(128)} %pad_add_fusion.1.where, bf16[128,2048]{1,0:T(8,128)(2,1)} %copy-done.9, bf16[128,2048]{1,0:T(8,128)(2,1)} %collective-permute-done.52.refs_1_, bf16[128,2048]{1,0:T(8,128)(2,1)} %copy-done.26, bf16[128,2048]{1,0:T(8,128)(2,1)} %copy-done.27), custom_call_target="tpu_custom_call" | custom-call | flops 1 | bytes 1 | tf_op jit(solution)/shard_map/assemble/pallas_call | solution.py:948
  (240 shorter events, 74.5 us)
Async XLA Ops:
  1.8 20.0 %collective-permute-start = (bf16[12,4,3072]{2,1,0:T(4,128)(2,1)S(1)}, bf16[12,4,3072]{2,1,0:T(4,128)(2,1)}, u32[]{:S(2)}, u32[]{:S(2)}) collective-permute-start(bf16[12,4,3072]{2,1,0:T(4,128)(2,1)S(1)} %pad_maximum_fusion.3.refs_0_), channel_id=1, source_target_pairs={{0,8},{8,0},{16,24},{24,16},{1,9},{9,1},{17,25},{25,17},{2,10},{10... | collective-permute-start | bytes 884744 | tf_op jit(solution)/shard_map/ppermute | solution.py:1047
  4.8 17.0 %collective-permute-start.1 = (bf16[12,4,3072]{2,1,0:T(4,128)(2,1)S(1)}, bf16[12,4,3072]{2,1,0:T(4,128)(2,1)}, u32[]{:S(2)}, u32[]{:S(2)}) collective-permute-start(bf16[12,4,3072]{2,1,0:T(4,128)(2,1)S(1)} %pad_maximum_fusion.3.refs_0_), channel_id=1, source_target_pairs={{0,16},{8,24},{16,0},{24,8},{1,17},{9,25},{17,1},{25,9},{2,18},{10... | collective-permute-start | bytes 884744 | tf_op jit(solution)/shard_map/ppermute | solution.py:1047
  6.3 15.5 %collective-permute-start.2 = (bf16[12,4,3072]{2,1,0:T(4,128)(2,1)S(1)}, bf16[12,4,3072]{2,1,0:T(4,128)(2,1)}, u32[]{:S(2)}, u32[]{:S(2)}) collective-permute-start(bf16[12,4,3072]{2,1,0:T(4,128)(2,1)S(1)} %pad_maximum_fusion.3.refs_0_), channel_id=1, source_target_pairs={{0,24},{8,16},{16,8},{24,0},{1,25},{9,17},{17,9},{25,1},{2,26},{10... | collective-permute-start | bytes 884744 | tf_op jit(solution)/shard_map/ppermute | solution.py:1047
  7.4 14.4 %collective-permute-start.3 = (bf16[512,512]{1,0:T(8,128)(2,1)S(1)}, bf16[512,512]{1,0:T(8,128)(2,1)S(1)}, u32[]{:S(2)}, u32[]{:S(2)}) collective-permute-start(bf16[512,512]{1,0:T(8,128)(2,1)S(1)} %dynamic-slice_bitcast_fusion), channel_id=1, source_target_pairs={{0,1},{1,0},{2,3},{3,2},{4,5},{5,4},{6,7},{7,6},{8,9},{9,8},{10,11... | collective-permute-start | bytes 1572872 | tf_op jit(solution)/shard_map/ppermute | solution.py:1047
  51.3 20.2 %collective-permute-start.6 = (bf16[1024,2048]{1,0:T(8,128)(2,1)}, bf16[1024,2048]{1,0:T(8,128)(2,1)}, u32[]{:S(2)}, u32[]{:S(2)}) collective-permute-start(bf16[1024,2048]{1,0:T(8,128)(2,1)} %get-tuple-element.248.h), channel_id=1, source_target_pairs={{0,1},{1,0},{2,3},{3,2},{4,5},{5,4},{6,7},{7,6},{8,9},{9,8},{10,11... | collective-permute-start | bytes 12582920 | tf_op jit(solution)/shard_map/ppermute | solution.py:1047
  51.8 19.7 %collective-permute-start.7 = (bf16[1024,512]{1,0:T(8,128)(2,1)}, bf16[1024,512]{1,0:T(8,128)(2,1)S(1)}, u32[]{:S(2)}, u32[]{:S(2)}) collective-permute-start(bf16[1024,512]{1,0:T(8,128)(2,1)} %get-tuple-element.249.a), channel_id=1, source_target_pairs={{0,1},{1,0},{2,3},{3,2},{4,5},{5,4},{6,7},{7,6},{8,9},{9,8},{10,11... | collective-permute-start | bytes 3145736 | tf_op jit(solution)/shard_map/ppermute | solution.py:1047
  59.7 10.8 %collective-permute-start.4 = (bf16[512,256]{1,0:T(8,128)(2,1)}, bf16[512,256]{1,0:T(8,128)(2,1)S(1)}, u32[]{:S(2)}, u32[]{:S(2)}) collective-permute-start(bf16[512,256]{1,0:T(8,128)(2,1)} %get-tuple-element.245.refs_3_), channel_id=1, source_target_pairs={{0,24},{8,16},{16,8},{24,0},{1,25},{9,17},{17,9},{25,1},{2,26},{10... | collective-permute-start | bytes 786440 | tf_op jit(solution)/shard_map/ppermute | solution.py:1047
  70.5 9.2 %collective-permute-start.5 = (bf16[512,256]{1,0:T(8,128)(2,1)}, bf16[512,256]{1,0:T(8,128)(2,1)S(1)}, u32[]{:S(2)}, u32[]{:S(2)}) collective-permute-start(bf16[512,256]{1,0:T(8,128)(2,1)} %get-tuple-element.247.refs_2_), channel_id=1, source_target_pairs={{0,16},{8,24},{16,0},{24,8},{1,17},{9,25},{17,1},{25,9},{2,18},{10... | collective-permute-start | bytes 786440 | tf_op jit(solution)/shard_map/ppermute | solution.py:1047
  79.7 10.6 %collective-permute-start.8 = (bf16[512,256]{1,0:T(8,128)(2,1)}, bf16[512,256]{1,0:T(8,128)(2,1)S(1)}, u32[]{:S(2)}, u32[]{:S(2)}) collective-permute-start(bf16[512,256]{1,0:T(8,128)(2,1)} %get-tuple-element.253.refs_1_), channel_id=1, source_target_pairs={{0,8},{8,0},{16,24},{24,16},{1,9},{9,1},{17,25},{25,17},{2,10},{10... | collective-permute-start | bytes 786440 | tf_op jit(solution)/shard_map/ppermute | solution.py:1047
  112.2 22.0 %collective-permute-start.9 = (bf16[4096,512]{1,0:T(8,128)(2,1)}, bf16[4096,512]{1,0:T(8,128)(2,1)}, u32[]{:S(2)}, u32[]{:S(2)}) collective-permute-start(bf16[4096,512]{1,0:T(8,128)(2,1)} %get-tuple-element.282.left), channel_id=1, source_target_pairs={{0,1},{1,0},{2,3},{3,2},{4,5},{5,4},{6,7},{7,6},{8,9},{9,8},{10,11... | collective-permute-start | bytes 12582920 | tf_op jit(solution)/shard_map/ppermute | solution.py:1047
  112.3 21.9 %collective-permute-start.10 = (bf16[512,2048]{1,0:T(8,128)(2,1)}, bf16[512,2048]{1,0:T(8,128)(2,1)S(1)}, u32[]{:S(2)}, u32[]{:S(2)}) collective-permute-start(bf16[512,2048]{1,0:T(8,128)(2,1)} %get-tuple-element.268.send_ref), channel_id=1, source_target_pairs={{0,1},{1,0},{2,3},{3,2},{4,5},{5,4},{6,7},{7,6},{8,9},{9,8},{10,11... | collective-permute-start | bytes 6291464 | tf_op jit(solution)/shard_map/ppermute | solution.py:1047
  112.8 21.4 %collective-permute-start.11 = (bf16[1024,512]{1,0:T(8,128)(2,1)}, bf16[1024,512]{1,0:T(8,128)(2,1)S(1)}, u32[]{:S(2)}, u32[]{:S(2)}) collective-permute-start(bf16[1024,512]{1,0:T(8,128)(2,1)} %get-tuple-element.269.h), channel_id=1, source_target_pairs={{0,1},{1,0},{2,3},{3,2},{4,5},{5,4},{6,7},{7,6},{8,9},{9,8},{10,11... | collective-permute-start | bytes 3145736 | tf_op jit(solution)/shard_map/ppermute | solution.py:1047
  112.8 21.3 %collective-permute-start.12 = (bf16[1024,512]{1,0:T(8,128)(2,1)}, bf16[1024,512]{1,0:T(8,128)(2,1)}, u32[]{:S(2)}, u32[]{:S(2)}) collective-permute-start(bf16[1024,512]{1,0:T(8,128)(2,1)} %get-tuple-element.270.m), channel_id=1, source_target_pairs={{0,1},{1,0},{2,3},{3,2},{4,5},{5,4},{6,7},{7,6},{8,9},{9,8},{10,11... | collective-permute-start | bytes 3145736 | tf_op jit(solution)/shard_map/ppermute | solution.py:1047
  134.2 4.9 %collective-permute-start.13 = (bf16[512,512]{1,0:T(8,128)(2,1)}, bf16[512,512]{1,0:T(8,128)(2,1)}, u32[]{:S(2)}, u32[]{:S(2)}) collective-permute-start(bf16[512,512]{1,0:T(8,128)(2,1)} %get-tuple-element.279), channel_id=1, source_target_pairs={{0,1},{1,0},{2,3},{3,2},{4,5},{5,4},{6,7},{7,6},{8,9},{9,8},{10,11... | collective-permute-start | bytes 1572872 | tf_op jit(solution)/shard_map/ppermute | solution.py:1047
  135.2 28.6 %all-to-all-start = ((bf16[4,512,256]{2,1,0:T(8,128)(2,1)}), bf16[4,512,256]{2,1,0:T(8,128)(2,1)S(1)}, u32[]{:S(2)}, u32[]{:S(2)}) async-start(bf16[4,512,256]{2,1,0:T(8,128)(2,1)} %get-tuple-element.291), calls=%async_computation | async-start | bytes 2097152 | tf_op jit(solution)/shard_map/all_to_all | solution.py:1055
  148.7 41.3 %collective-permute-start.14 = (bf16[1024,512]{1,0:T(8,128)(2,1)}, bf16[1024,512]{1,0:T(8,128)(2,1)}, u32[]{:S(2)}, u32[]{:S(2)}) collective-permute-start(bf16[1024,512]{1,0:T(8,128)(2,1)} %get-tuple-element.304), channel_id=1, source_target_pairs={{0,16},{8,24},{16,0},{24,8},{1,17},{9,25},{17,1},{25,9},{2,18},{10... | collective-permute-start | bytes 3145736 | tf_op jit(solution)/shard_map/ppermute | solution.py:1047
  150.7 39.3 %collective-permute-start.15 = (bf16[1024,512]{1,0:T(8,128)(2,1)}, bf16[1024,512]{1,0:T(8,128)(2,1)}, u32[]{:S(2)}, u32[]{:S(2)}) collective-permute-start(bf16[1024,512]{1,0:T(8,128)(2,1)} %get-tuple-element.305), channel_id=1, source_target_pairs={{0,8},{8,0},{16,24},{24,16},{1,9},{9,1},{17,25},{25,17},{2,10},{10... | collective-permute-start | bytes 3145736 | tf_op jit(solution)/shard_map/ppermute | solution.py:1047
  163.7 64.8 %collective-permute-start.17 = (bf16[1024,1280]{1,0:T(8,128)(2,1)}, bf16[1024,1280]{1,0:T(8,128)(2,1)}, u32[]{:S(2)}, u32[]{:S(2)}) collective-permute-start(bf16[1024,1280]{1,0:T(8,128)(2,1)} %get-tuple-element.313), channel_id=1, source_target_pairs={{0,2},{2,0},{4,6},{6,4},{1,3},{3,1},{5,7},{7,5},{8,10},{10,8},{12,... | collective-permute-start | bytes 7864328 | tf_op jit(solution)/shard_map/ppermute | solution.py:1047
  193.3 35.3 %collective-permute-start.16 = (bf16[2048,384]{1,0:T(8,128)(2,1)}, bf16[2048,384]{1,0:T(8,128)(2,1)S(1)}, u32[]{:S(2)}, u32[]{:S(2)}) collective-permute-start(bf16[2048,384]{1,0:T(8,128)(2,1)} %attend_back.2.refs_0_), channel_id=1, source_target_pairs={{0,1},{1,0},{2,3},{3,2},{4,5},{5,4},{6,7},{7,6},{8,9},{9,8},{10,11... | collective-permute-start | bytes 4718600 | tf_op jit(solution)/shard_map/ppermute | solution.py:1047
  193.3 35.2 %all-to-all-start.1 = ((bf16[4,512,384]{2,1,0:T(8,128)(2,1)}), bf16[4,512,384]{2,1,0:T(8,128)(2,1)S(1)}, u32[]{:S(2)}, u32[]{:S(2)}) async-start(bf16[4,512,384]{2,1,0:T(8,128)(2,1)} %bitcast.13), calls=%async_computation.1 | async-start | bytes 3145728 | tf_op jit(solution)/shard_map/all_to_all | solution.py:1055
  197.0 31.5 %collective-permute-start.18 = (bf16[512,512]{1,0:T(8,128)(2,1)}, bf16[512,512]{1,0:T(8,128)(2,1)}, u32[]{:S(2)}, u32[]{:S(2)}) collective-permute-start(bf16[512,512]{1,0:T(8,128)(2,1)} %get-tuple-element.314), channel_id=1, source_target_pairs={{0,8},{8,0},{16,24},{24,16},{1,9},{9,1},{17,25},{25,17},{2,10},{10... | collective-permute-start | bytes 1572872 | tf_op jit(solution)/shard_map/ppermute | solution.py:1047
  199.1 29.4 %collective-permute-start.19 = (bf16[512,512]{1,0:T(8,128)(2,1)}, bf16[512,512]{1,0:T(8,128)(2,1)}, u32[]{:S(2)}, u32[]{:S(2)}) collective-permute-start(bf16[512,512]{1,0:T(8,128)(2,1)} %get-tuple-element.315), channel_id=1, source_target_pairs={{0,16},{8,24},{16,0},{24,8},{1,17},{9,25},{17,1},{25,9},{2,18},{10... | collective-permute-start | bytes 1572872 | tf_op jit(solution)/shard_map/ppermute | solution.py:1047
  228.6 12.3 %collective-permute-start.20 = (bf16[2048,384]{1,0:T(8,128)(2,1)}, bf16[2048,384]{1,0:T(8,128)(2,1)}, u32[]{:S(2)}, u32[]{:S(2)}) collective-permute-start(bf16[2048,384]{1,0:T(8,128)(2,1)} %attend_back.3.refs_1_), channel_id=1, source_target_pairs={{0,1},{1,0},{2,3},{3,2},{4,5},{5,4},{6,7},{7,6},{8,9},{9,8},{10,11... | collective-permute-start | bytes 4718600 | tf_op jit(solution)/shard_map/ppermute | solution.py:1047
  229.8 23.0 %all-to-all-start.2 = ((bf16[4,512,384]{2,1,0:T(8,128)(2,1)}), bf16[4,512,384]{2,1,0:T(8,128)(2,1)S(1)}, u32[]{:S(2)}, u32[]{:S(2)}) async-start(bf16[4,512,384]{2,1,0:T(8,128)(2,1)} %bitcast.42), calls=%async_computation.2 | async-start | bytes 3145728 | tf_op jit(solution)/shard_map/all_to_all | solution.py:1055
  235.8 16.9 %collective-permute-start.21 = (bf16[512,512]{1,0:T(8,128)(2,1)}, bf16[512,512]{1,0:T(8,128)(2,1)}, u32[]{:S(2)}, u32[]{:S(2)}) collective-permute-start(bf16[512,512]{1,0:T(8,128)(2,1)} %get-tuple-element.328), channel_id=1, source_target_pairs={{0,2},{2,0},{4,6},{6,4},{1,3},{3,1},{5,7},{7,5},{8,10},{10,8},{12,... | collective-permute-start | bytes 1572872 | tf_op jit(solution)/shard_map/ppermute | solution.py:1047
  254.2 18.6 %collective-permute-start.23 = (bf16[256,1280]{1,0:T(8,128)(2,1)}, bf16[256,1280]{1,0:T(8,128)(2,1)}, u32[]{:S(2)}, u32[]{:S(2)}) collective-permute-start(bf16[256,1280]{1,0:T(8,128)(2,1)} %get-tuple-element.340), channel_id=1, source_target_pairs={{0,16},{8,24},{16,0},{24,8},{1,17},{9,25},{17,1},{25,9},{2,18},{10... | collective-permute-start | bytes 1966088 | tf_op jit(solution)/shard_map/ppermute | solution.py:1047
  255.7 17.1 %collective-permute-start.24 = (bf16[256,1280]{1,0:T(8,128)(2,1)}, bf16[256,1280]{1,0:T(8,128)(2,1)}, u32[]{:S(2)}, u32[]{:S(2)}) collective-permute-start(bf16[256,1280]{1,0:T(8,128)(2,1)} %get-tuple-element.341), channel_id=1, source_target_pairs={{0,8},{8,0},{16,24},{24,16},{1,9},{9,1},{17,25},{25,17},{2,10},{10... | collective-permute-start | bytes 1966088 | tf_op jit(solution)/shard_map/ppermute | solution.py:1047
  256.2 16.6 %collective-permute-start.22 = (bf16[256,512]{1,0:T(8,128)(2,1)S(1)}, bf16[256,512]{1,0:T(8,128)(2,1)S(1)}, u32[]{:S(2)}, u32[]{:S(2)}) collective-permute-start(bf16[256,512]{1,0:T(8,128)(2,1)S(1)} %add_convert_fusion.20), channel_id=1, source_target_pairs={{0,6},{2,4},{4,2},{6,0},{1,7},{3,5},{5,3},{7,1},{8,14},{10,12},{12... | collective-permute-start | bytes 786440 | tf_op jit(solution)/shard_map/ppermute | solution.py:1047
  276.2 11.4 %collective-permute-start.25 = (bf16[512,512]{1,0:T(8,128)(2,1)}, bf16[512,512]{1,0:T(8,128)(2,1)S(1)}, u32[]{:S(2)}, u32[]{:S(2)}) collective-permute-start(bf16[512,512]{1,0:T(8,128)(2,1)} %get-tuple-element.354), channel_id=1, source_target_pairs={{0,1},{1,0},{2,3},{3,2},{4,5},{5,4},{6,7},{7,6},{8,9},{9,8},{10,11... | collective-permute-start | bytes 1572872 | tf_op jit(solution)/shard_map/ppermute | solution.py:1047
  276.2 10.1 %collective-permute-start.26 = (bf16[128,1280]{1,0:T(8,128)(2,1)S(1)}, bf16[128,1280]{1,0:T(8,128)(2,1)S(1)}, u32[]{:S(2)}, u32[]{:S(2)}) collective-permute-start(bf16[128,1280]{1,0:T(8,128)(2,1)S(1)} %add_convert_fusion.15), channel_id=1, source_target_pairs={{0,8},{8,0},{16,24},{24,16},{1,9},{9,1},{17,25},{25,17},{2,10},{10... | collective-permute-start | bytes 983048 | tf_op jit(solution)/shard_map/ppermute | solution.py:1047
  277.8 9.8 %collective-permute-start.27 = (bf16[128,1280]{1,0:T(8,128)(2,1)S(1)}, bf16[128,1280]{1,0:T(8,128)(2,1)S(1)}, u32[]{:S(2)}, u32[]{:S(2)}) collective-permute-start(bf16[128,1280]{1,0:T(8,128)(2,1)S(1)} %add_convert_fusion.14), channel_id=1, source_target_pairs={{0,16},{8,24},{16,0},{24,8},{1,17},{9,25},{17,1},{25,9},{2,18},{10... | collective-permute-start | bytes 983048 | tf_op jit(solution)/shard_map/ppermute | solution.py:1047
  278.4 20.4 %collective-permute-start.30 = (bf16[256,512]{1,0:T(8,128)(2,1)S(1)}, bf16[256,512]{1,0:T(8,128)(2,1)}, u32[]{:S(2)}, u32[]{:S(2)}) collective-permute-start(bf16[256,512]{1,0:T(8,128)(2,1)S(1)} %add_convert_fusion.19), channel_id=1, source_target_pairs={{0,6},{2,4},{4,2},{6,0},{1,7},{3,5},{5,3},{7,1},{8,14},{10,12},{12... | collective-permute-start | bytes 786440 | tf_op jit(solution)/shard_map/ppermute | solution.py:1047
  290.9 7.8 %collective-permute-start.29 = (bf16[128,640]{1,0:T(8,128)(2,1)S(1)}, bf16[128,640]{1,0:T(8,128)(2,1)S(1)}, u32[]{:S(2)}, u32[]{:S(2)}) collective-permute-start(bf16[128,640]{1,0:T(8,128)(2,1)S(1)} %slice.138), channel_id=1, source_target_pairs={{0,8},{8,0},{16,24},{24,16},{1,9},{9,1},{17,25},{25,17},{2,10},{10... | collective-permute-start | bytes 491528 | tf_op jit(solution)/shard_map/ppermute | solution.py:1047
  291.5 11.8 %collective-permute-start.32 = (bf16[128,1280]{1,0:T(8,128)(2,1)S(1)}, bf16[128,1280]{1,0:T(8,128)(2,1)S(1)}, u32[]{:S(2)}, u32[]{:S(2)}) collective-permute-start(bf16[128,1280]{1,0:T(8,128)(2,1)S(1)} %fusion.3), channel_id=1, source_target_pairs={{0,6},{2,4},{4,2},{6,0},{1,7},{3,5},{5,3},{7,1},{8,14},{10,12},{12... | collective-permute-start | bytes 983048 | tf_op jit(solution)/shard_map/ppermute | solution.py:1047
  304.1 25.0 %all-to-all-start.3 = ((bf16[4,256,896]{2,1,0:T(8,128)(2,1)}), bf16[4,256,896]{2,1,0:T(8,128)(2,1)S(1)}, u32[]{:S(2)}, u32[]{:S(2)}) async-start(bf16[4,256,896]{2,1,0:T(8,128)(2,1)} %last_grad.1), calls=%async_computation.3 | async-start | bytes 3670016 | tf_op jit(solution)/shard_map/all_to_all | solution.py:1055
  309.2 23.7 %collective-permute-start.34 = (bf16[128,1280]{1,0:T(8,128)(2,1)S(1)}, bf16[128,1280]{1,0:T(8,128)(2,1)}, u32[]{:S(2)}, u32[]{:S(2)}) collective-permute-start(bf16[128,1280]{1,0:T(8,128)(2,1)S(1)} %add_convert_fusion.8), channel_id=1, source_target_pairs={{0,6},{2,4},{4,2},{6,0},{1,7},{3,5},{5,3},{7,1},{8,14},{10,12},{12... | collective-permute-start | bytes 983048 | tf_op jit(solution)/shard_map/ppermute | solution.py:1047
  310.9 24.1 %collective-permute-start.36 = (bf16[512,512]{1,0:T(8,128)(2,1)S(1)}, bf16[512,512]{1,0:T(8,128)(2,1)S(1)}, u32[]{:S(2)}, u32[]{:S(2)}) collective-permute-start(bf16[512,512]{1,0:T(8,128)(2,1)S(1)} %pad_maximum_fusion.1.refs_0_), channel_id=1, source_target_pairs={{0,2},{2,0},{4,6},{6,4},{1,3},{3,1},{5,7},{7,5},{8,10},{10,8},{12,... | collective-permute-start | bytes 1572872 | tf_op jit(solution)/shard_map/ppermute | solution.py:1047
  315.4 17.5 %collective-permute-start.33 = (bf16[64,640]{1,0:T(8,128)(2,1)S(1)}, bf16[64,640]{1,0:T(8,128)(2,1)S(1)}, u32[]{:S(2)}, u32[]{:S(2)}) collective-permute-start(bf16[64,640]{1,0:T(8,128)(2,1)S(1)} %add_convert_fusion.25), channel_id=1, source_target_pairs={{0,2},{2,0},{4,6},{6,4},{1,3},{3,1},{5,7},{7,5},{8,10},{10,8},{12,... | collective-permute-start | bytes 245768 | tf_op jit(solution)/shard_map/ppermute | solution.py:1047
  332.9 6.3 %collective-permute-start.35 = (bf16[64,640]{1,0:T(8,128)(2,1)S(1)}, bf16[64,640]{1,0:T(8,128)(2,1)S(1)}, u32[]{:S(2)}, u32[]{:S(2)}) collective-permute-start(bf16[64,640]{1,0:T(8,128)(2,1)S(1)} %add_convert_fusion.24), channel_id=1, source_target_pairs={{0,6},{2,4},{4,2},{6,0},{1,7},{3,5},{5,3},{7,1},{8,14},{10,12},{12... | collective-permute-start | bytes 245768 | tf_op jit(solution)/shard_map/ppermute | solution.py:1047
  340.5 16.2 %collective-permute-start.40 = (bf16[128,2048]{1,0:T(8,128)(2,1)}, bf16[128,2048]{1,0:T(8,128)(2,1)S(1)}, u32[]{:S(2)}, u32[]{:S(2)}) collective-permute-start(bf16[128,2048]{1,0:T(8,128)(2,1)} %get-tuple-element.400), channel_id=1, source_target_pairs={{0,2},{2,0},{4,6},{6,4},{1,3},{3,1},{5,7},{7,5},{8,10},{10,8},{12,... | collective-permute-start | bytes 1572872 | tf_op jit(solution)/shard_map/ppermute | solution.py:1047
  358.0 8.3 %collective-permute-start.41 = (bf16[64,1152]{1,0:T(8,128)(2,1)S(1)}, bf16[64,1152]{1,0:T(8,128)(2,1)S(1)}, u32[]{:S(2)}, u32[]{:S(2)}) collective-permute-start(bf16[64,1152]{1,0:T(8,128)(2,1)S(1)} %pad_maximum_fusion.4.refs_0_), channel_id=1, source_target_pairs={{0,8},{8,0},{16,24},{24,16},{1,9},{9,1},{17,25},{25,17},{2,10},{10... | collective-permute-start | bytes 442376 | tf_op jit(solution)/shard_map/ppermute | solution.py:1047
  359.5 8.7 %collective-permute-start.42 = (bf16[64,1152]{1,0:T(8,128)(2,1)S(1)}, bf16[64,1152]{1,0:T(8,128)(2,1)}, u32[]{:S(2)}, u32[]{:S(2)}) collective-permute-start(bf16[64,1152]{1,0:T(8,128)(2,1)S(1)} %pad_maximum_fusion.4.refs_0_), channel_id=1, source_target_pairs={{0,16},{8,24},{16,0},{24,8},{1,17},{9,25},{17,1},{25,9},{2,18},{10... | collective-permute-start | bytes 442376 | tf_op jit(solution)/shard_map/ppermute | solution.py:1047
  360.0 8.1 %collective-permute-start.43 = (bf16[64,1152]{1,0:T(8,128)(2,1)S(1)}, bf16[64,1152]{1,0:T(8,128)(2,1)}, u32[]{:S(2)}, u32[]{:S(2)}) collective-permute-start(bf16[64,1152]{1,0:T(8,128)(2,1)S(1)} %pad_maximum_fusion.4.refs_0_), channel_id=1, source_target_pairs={{0,24},{8,16},{16,8},{24,0},{1,25},{9,17},{17,9},{25,1},{2,26},{10... | collective-permute-start | bytes 442376 | tf_op jit(solution)/shard_map/ppermute | solution.py:1047
  361.5 12.8 %collective-permute-start.44 = (bf16[64,2048]{1,0:T(8,128)(2,1)S(1)}, bf16[64,2048]{1,0:T(8,128)(2,1)S(1)}, u32[]{:S(2)}, u32[]{:S(2)}) collective-permute-start(bf16[64,2048]{1,0:T(8,128)(2,1)S(1)} %add_convert_fusion.17), channel_id=1, source_target_pairs={{0,6},{2,4},{4,2},{6,0},{1,7},{3,5},{5,3},{7,1},{8,14},{10,12},{12... | collective-permute-start | bytes 786440 | tf_op jit(solution)/shard_map/ppermute | solution.py:1047
  365.3 25.1 %collective-permute-start.49 = (bf16[256,1280]{1,0:T(8,128)(2,1)S(1)}, bf16[256,1280]{1,0:T(8,128)(2,1)S(1)}, u32[]{:S(2)}, u32[]{:S(2)}) collective-permute-start(bf16[256,1280]{1,0:T(8,128)(2,1)S(1)} %pad_maximum_fusion.refs_0_), channel_id=1, source_target_pairs={{0,2},{2,0},{4,6},{6,4},{1,3},{3,1},{5,7},{7,5},{8,10},{10,8},{12,... | collective-permute-start | bytes 1966088 | tf_op jit(solution)/shard_map/ppermute | solution.py:1047
  375.4 15.0 %collective-permute-start.48 = (bf16[64,2048]{1,0:T(8,128)(2,1)S(1)}, bf16[64,2048]{1,0:T(8,128)(2,1)S(1)}, u32[]{:S(2)}, u32[]{:S(2)}) collective-permute-start(bf16[64,2048]{1,0:T(8,128)(2,1)S(1)} %add_convert_fusion.16), channel_id=1, source_target_pairs={{0,6},{2,4},{4,2},{6,0},{1,7},{3,5},{5,3},{7,1},{8,14},{10,12},{12... | collective-permute-start | bytes 786440 | tf_op jit(solution)/shard_map/ppermute | solution.py:1047
  380.0 5.2 %collective-permute-start.47 = (bf16[4,12,512]{2,1,0:T(8,128)(2,1)S(1)}, bf16[4,12,512]{2,1,0:T(8,128)(2,1)S(1)}, u32[]{:S(2)}, u32[]{:S(2)}) collective-permute-start(bf16[4,12,512]{2,1,0:T(8,128)(2,1)S(1)} %bitcast.55), channel_id=1, source_target_pairs={{0,24},{8,16},{16,8},{24,0},{1,25},{9,17},{17,9},{25,1},{2,26},{10... | collective-permute-start | bytes 147464 | tf_op jit(solution)/shard_map/ppermute | solution.py:1047
  391.0 14.0 %collective-permute-start.52 = (bf16[128,2048]{1,0:T(8,128)(2,1)S(1)}, bf16[128,2048]{1,0:T(8,128)(2,1)}, u32[]{:S(2)}, u32[]{:S(2)}) collective-permute-start(bf16[128,2048]{1,0:T(8,128)(2,1)S(1)} %pad_maximum_fusion.2.refs_0_), channel_id=1, source_target_pairs={{0,2},{2,0},{4,6},{6,4},{1,3},{3,1},{5,7},{7,5},{8,10},{10,8},{12,... | collective-permute-start | bytes 1572872 | tf_op jit(solution)/shard_map/ppermute | solution.py:1047
  (57 other events, 524.0 us)
where the time goes:
time: 423 us; the launch traced here: 416 us
  Pallas kernels  236 us (56%)
  starting transfers between devices  74.1 us (18%)
  waiting for transfers between devices  52.3 us (12%)
  other arithmetic  25.3 us (6%)
  local copies, waits for them, and re-layouts  13.6 us (3%)
  matrix products  12.1 us (3%)
    ppermute x55, starting transfers between devices, swap(): return lax.ppermute(value, axis, [(i, i ^ bits) for i in range(size)])  59 us
    pallas_call x2, Pallas kernels, attend_back(): pl.pallas_call(partial(attend_back_kernel, chunk=min(chunk, seq), groups=...  49.2 us
    ppermute x55, waiting for transfers between devices, swap(): return lax.ppermute(value, axis, [(i, i ^ bits) for i in range(size)])  36.6 us
    pallas_call x4, Pallas kernels, attend(): pl.pallas_call(attend_kernel, grid_spec=spec, out_shape=[jax.ShapeDtypeSt...  31.7 us
    pallas_call x1, Pallas kernels, front(): pl.pallas_call(front_kernel, grid_spec=spec, out_shape=[jax.ShapeDtypeStr...  23.4 us
    pallas_call x1, Pallas kernels, inner_part(): pl.pallas_call(inner_kernel, grid_spec=spec, out_shape=[shape_of(rows, in...  21.1 us
    pallas_call x1, Pallas kernels, outer_part(): pl.pallas_call(outer_kernel, grid_spec=spec, out_shape=[shape_of(rows, wi...  20.9 us
    convert_element_type x16, other arithmetic, add(): return (a.astype(f32) + b.astype(f32)).astype(bf16)  17 us
  transfers between devices with their start and end apart: 59, of which 16 were waited for; matrix products, arithmetic and copies ran while one was open for 9% of the time, Pallas kernels for 43%

commit v1 on v0

--- a/solution.py
+++ b/solution.py
@@ -760,7 +760,7 @@
 
 
 def join_kernel(core, first_ref, second_ref, wq, wk, wv, resid_ref, gain_ref, gres_ref, out_ref, *refs):
-    ga_ref, ga_send_ref, gatt_ref, ggain_ref, sum_ref, total = refs
+    ga_ref, ga_send_ref, gatt_ref, ggain_ref, sum_ref, total, resid_rows, gres_rows = refs
     i = pl.program_id(0)
     pair = 2 * HEAD_DIM
 
@@ -768,6 +768,10 @@
     def _():
         total[...] = jnp.zeros_like(total)
 
+    deep = resid_ref.shape[0]
+    here = pl.ds(pl.multiple_of(i * deep, deep), deep)
+    resid_rows[here, :] = resid_ref[...]
+    gres_rows[here, :] = gres_ref[...]
     spans = [slice(t * pair, (t + 1) * pair) for t in range(3)]
     left = jnp.concatenate([ref[:, span] for span in spans for ref in (first_ref, second_ref)], axis=1)
     weights = jnp.concatenate([wq[...], wk[...], wv[...]], axis=1)
@@ -775,7 +779,7 @@
 
     @pl.when(i == pl.num_programs(0) - 1)
     def _():
-        resid = resid_ref[...]
+        resid = resid_rows[...]
         centered = resid - jnp.mean(resid, axis=1, keepdims=True)
         scale = lax.rsqrt(jnp.mean(centered * centered, axis=1, keepdims=True) + epsilon)
         plain = centered * scale
@@ -784,7 +788,7 @@
         grad = grad * gain_ref[...]
         first = jnp.mean(grad, axis=1, keepdims=True)
         second = jnp.mean(grad * plain, axis=1, keepdims=True)
-        gres = gres_ref[...] + scale * (grad - first - plain * second)
+        gres = gres_rows[...] + scale * (grad - first - plain * second)
         sum_ref[...] = jnp.sum(gres, axis=0, keepdims=True)
         ga = gres.astype(bf16)
         ga_ref[...] = ga
@@ -811,9 +815,9 @@
             pl.BlockSpec((width, own), lambda i, c: (0, i)),
             pl.BlockSpec((width, own), lambda i, c: (0, groups + i)),
             pl.BlockSpec((width, own), lambda i, c: (0, 2 * groups + i)),
-            whole(rows, width),
+            pl.BlockSpec((rows // groups, width), lambda i, c: (i, 0)),
             whole(1, width),
-            whole(rows, width),
+            pl.BlockSpec((rows // groups, width), lambda i, c: (i, 0)),
             whole(width, width),
         ],
         out_specs=[
@@ -823,7 +827,7 @@
             whole(1, width),
             whole(1, width),
         ],
-        scratch_shapes=[pltpu.VMEM((rows, width), f32)],
+        scratch_shapes=[pltpu.VMEM((rows, width), f32)] * 3,
     )
     return pl.pallas_call(
         join_kernel,

time: 423 us -> 423 us (level)
  no operation moved by 1% of the time
where the time goes in v1:
time: 423 us; the launch traced here: 416 us
  Pallas kernels  236 us (56%)
  starting transfers between devices  74.8 us (18%)
  waiting for transfers between devices  51.6 us (12%)
  other arithmetic  25.3 us (6%)
  local copies, waits for them, and re-layouts  13.6 us (3%)
  matrix products  12.1 us (3%)
    ppermute x55, starting transfers between devices, swap(): return lax.ppermute(value, axis, [(i, i ^ bits) for i in range(size)])  59.7 us
    pallas_call x2, Pallas kernels, attend_back(): pl.pallas_call(partial(attend_back_kernel, chunk=min(chunk, seq), groups=...  49.2 us
    ppermute x55, waiting for transfers between devices, swap(): return lax.ppermute(value, axis, [(i, i ^ bits) for i in range(size)])  36 us
    pallas_call x4, Pallas kernels, attend(): pl.pallas_call(attend_kernel, grid_spec=spec, out_shape=[jax.ShapeDtypeSt...  31.7 us
    pallas_call x1, Pallas kernels, front(): pl.pallas_call(front_kernel, grid_spec=spec, out_shape=[jax.ShapeDtypeStr...  23.4 us
    pallas_call x1, Pallas kernels, inner_part(): pl.pallas_call(inner_kernel, grid_spec=spec, out_shape=[shape_of(rows, in...  21.1 us
    pallas_call x1, Pallas kernels, outer_part(): pl.pallas_call(outer_kernel, grid_spec=spec, out_shape=[shape_of(rows, wi...  20.9 us
    convert_element_type x16, other arithmetic, add(): return (a.astype(f32) + b.astype(f32)).astype(bf16)  17 us
  transfers between devices with their start and end apart: 59, of which 16 were waited for; matrix products, arithmetic and copies ran while one was open for 9% of the time, Pallas kernels for 43%

profile of v1, /device:TPU:0, one launch (start us, length us, event | category | flops | bytes accessed | tf_op | source)
XLA Modules:
  0.0 415.5 jit_solution(14981910569435588001)
XLA Ops:
  1.8 3.0 collective-permute-start
  7.5 10.4 %convolution_convert_fusion.ga_ref = bf16[512,4096]{1,0:T(8,128)(2,1)} fusion(bf16[4096,1024]{1,0:T(8,128)(2,1)} %w2_ref.1, bf16[1,512,1024]{2,1,0:T(8,128)(2,1)} %param.35), kind=kOutput, calls=%fused_computation | convolution fusion | flops 4297064448 | bytes 13631488 | tf_op jit(solution)/shard_map/dot_general | solution.py:1150
  21.8 6.1 %prepare.1 = (f32[4,48,2048]{2,1,0:T(8,128)}, f32[5,48,128]{2,1,0:T(8,128)}, bf16[240,1024]{1,0:T(8,128)(2,1)}, bf16[1024,240]{1,0:T(8,128)(2,1)}, bf16[256,1024]{1,0:T(8,128)(2,1)}) custom-call(bf16[12,4,3072]{2,1,0:T(4,128)(2,1)} %copy-done.13, bf16[12,4,3072]{2,1,0:T(4,128)(2,1)} %collective-permute-done.refs_1_, ...), custom_call_target="tpu_custom_call" | custom-call | flops 1 | bytes 1 | tf_op jit(solution)/shard_map/prepare/pallas_call | solution.py:79
  27.8 23.4 %front.1 = (bf16[1024,2048]{1,0:T(8,128)(2,1)}, bf16[2048,768]{1,0:T(8,128)(2,1)}, f32[512,1024]{1,0:T(8,128)}, bf16[1024,512]{1,0:T(8,128)(2,1)}) custom-call(s32[1]{0:T(128)} %bitcast.member, s32[1]{0:T(128)S(6)} %copy.56.bucket, f32[4,48,2048]{2,1,0:T(8,128)} %get-tuple-element.238.pixel_ref, f32[5,48,128]{2,1,0:T(8,128)} %get-tuple-element.239.key_ref, ...), custom_call_target="tpu_custom_call" | custom-call | flops 1 | bytes 1 | tf_op jit(solution)/shard_map/front/pallas_call | solution.py:166
  51.9 7.8 %attend.4 = (bf16[512,256]{1,0:T(8,128)(2,1)}, f32[2,2,512]{2,1,0:T(2,128)}) custom-call(s32[1]{0:T(128)} %bitcast.member, bf16[2048,768]{1,0:T(8,128)(2,1)} %get-tuple-element.312.q_ref.k_ref.v_ref, bf16[2048,768]{1,0:T(8,128)(2,1)} %get-tuple-element.312.q_ref.k_ref.v_ref, bf16[2048,768]{1,0:T(8,128)(2,1)} %get-tuple-element.312.q_ref.k_ref.v_ref), custom_call_target="tpu_custom_call" | custom-call | flops 1 | bytes 1 | tf_op jit(solution)/shard_map/attend/pallas_call | solution.py:228
  59.7 2.9 collective-permute-start.4
  62.7 7.8 %attend.5 = (bf16[512,256]{1,0:T(8,128)(2,1)}, f32[2,2,512]{2,1,0:T(2,128)}) custom-call(s32[1]{0:T(128)} %bitcast.member, bf16[2048,768]{1,0:T(8,128)(2,1)} %get-tuple-element.312.q_ref.k_ref.v_ref, bf16[2048,768]{1,0:T(8,128)(2,1)} %get-tuple-element.312.q_ref.k_ref.v_ref, bf16[2048,768]{1,0:T(8,128)(2,1)} %get-tuple-element.312.q_ref.k_ref.v_ref), custom_call_target="tpu_custom_call" | custom-call | flops 1 | bytes 1 | tf_op jit(solution)/shard_map/attend/pallas_call | solution.py:228
  71.5 8.2 %attend.6 = (bf16[512,256]{1,0:T(8,128)(2,1)}, f32[2,2,512]{2,1,0:T(2,128)}) custom-call(s32[1]{0:T(128)} %bitcast.member, bf16[2048,768]{1,0:T(8,128)(2,1)} %get-tuple-element.312.q_ref.k_ref.v_ref, bf16[2048,768]{1,0:T(8,128)(2,1)} %get-tuple-element.312.q_ref.k_ref.v_ref, bf16[2048,768]{1,0:T(8,128)(2,1)} %get-tuple-element.312.q_ref.k_ref.v_ref), custom_call_target="tpu_custom_call" | custom-call | flops 1 | bytes 1 | tf_op jit(solution)/shard_map/attend/pallas_call | solution.py:228
  82.5 7.8 %attend.7 = (bf16[512,256]{1,0:T(8,128)(2,1)}, f32[2,2,512]{2,1,0:T(2,128)}) custom-call(s32[1]{0:T(128)} %bitcast.member, bf16[2048,768]{1,0:T(8,128)(2,1)} %get-tuple-element.312.q_ref.k_ref.v_ref, bf16[2048,768]{1,0:T(8,128)(2,1)} %get-tuple-element.312.q_ref.k_ref.v_ref, bf16[2048,768]{1,0:T(8,128)(2,1)} %get-tuple-element.312.q_ref.k_ref.v_ref), custom_call_target="tpu_custom_call" | custom-call | flops 1 | bytes 1 | tf_op jit(solution)/shard_map/attend/pallas_call | solution.py:228
  91.0 21.1 %inner_part.1 = (bf16[512,4096]{1,0:T(8,128)(2,1)}, bf16[4096,512]{1,0:T(8,128)(2,1)}, bf16[512,2048]{1,0:T(8,128)(2,1)}, bf16[512,2048]{1,0:T(8,128)(2,1)}, f32...) custom-call(s32[1]{0:T(128)} %bitcast.member, s32[1]{0:T(128)} %bitcast.1.core, ...), custom_call_target="tpu_custom_call" | custom-call | flops 1 | bytes 1 | tf_op jit(solution)/shard_map/inner_part/pallas_call | solution.py:507
  113.3 20.9 %outer_part.1 = (bf16[512,1024]{1,0:T(8,128)(2,1)}, f32[512,1024]{1,0:T(8,128)}, bf16[512,1024]{1,0:T(8,128)(2,1)}, bf16[512,512]{1,0:T(8,128)(2,1)}, bf16[4,512,256]{2,1,0:T(8,128)(2,1)}, /*index=5*/f32[1,1024]{1,0:T(1,128)}) custom-call(s32[1]{0:T(128)} %bitcast.1.core, bf16[512,4096]{1,0:T(8,128)(2,1)} %get-tuple-element.271.act_ref, ...), custom_call_target="tpu_custom_call" | custom-call | flops 1 | bytes 1 | tf_op jit(solution)/shard_map/outer_part/pallas_call | solution.py:593
  135.2 4.0 all-to-all-start
  139.2 9.6 %out_grad.1 = (bf16[1024,512]{1,0:T(8,128)(2,1)}, bf16[1024,512]{1,0:T(8,128)(2,1)}, bf16[1024,512]{1,0:T(8,128)(2,1)}, bf16[1024,512]{1,0:T(8,128)(2,1)}) custom-call(s32[1]{0:T(128)} %bitcast.1.core, bf16[4096,512]{1,0:T(8,128)(2,1)} %get-tuple-element.282.left, bf16[4096,512]{1,0:T(8,128)(2,1)} %collective-permute-done.9.left_other, ...), custom_call_target="tpu_custom_call" | custom-call | flops 1 | bytes 1 | tf_op jit(solution)/shard_map/out_grad/pallas_call | solution.py:639
  152.2 11.5 %in_grad.1 = (bf16[1024,1280]{1,0:T(8,128)(2,1)}, bf16[1024,1280]{1,0:T(8,128)(2,1)}) custom-call(s32[1]{0:T(128)} %bitcast.1.core, s32[1]{0:T(128)} %bitcast.11.high, bf16[1024,512]{1,0:T(8,128)(2,1)} %get-tuple-element.269.h, bf16[1024,512]{1,0:T(8,128)(2,1)} %copy-done.15, bf16[512,2048]{1,0:T(8,128)(2,1)} %get-tuple-element.272.keep_ref.u, ...), custom_call_target="tpu_custom_call" | custom-call | flops 1 | bytes 1 | tf_op jit(solution)/shard_map/in_grad/pallas_call | solution.py:692
  165.4 24.6 %attend_back.2.refs_0_ = bf16[2048,384]{1,0:T(8,128)(2,1)} custom-call(s32[1]{0:T(128)} %bitcast.member, bf16[2048,768]{1,0:T(8,128)(2,1)} %get-tuple-element.312.q_ref.k_ref.v_ref, bf16[2048,768]{1,0:T(8,128)(2,1)} %get-tuple-element.312.q_ref.k_ref.v_ref, bf16[2048,768]{1,0:T(8,128)(2,1)} %get-tuple-element.312.q_ref.k_ref.v_ref, ...), custom_call_target="tpu_custom_call" | custom-call | flops 1 | bytes 1 | tf_op jit(solution)/shard_map/attend_back/pallas_call | solution.py:310
  190.1 3.2 add_convert_fusion.4
  193.3 3.7 all-to-all-start.1
  197.0 2.1 collective-permute-start.18
  200.6 24.6 %attend_back.3.refs_1_ = bf16[2048,384]{1,0:T(8,128)(2,1)} custom-call(s32[1]{0:T(128)} %bitcast.member, bf16[2048,768]{1,0:T(8,128)(2,1)} %get-tuple-element.312.q_ref.k_ref.v_ref, bf16[2048,768]{1,0:T(8,128)(2,1)} %get-tuple-element.312.q_ref.k_ref.v_ref, bf16[2048,768]{1,0:T(8,128)(2,1)} %get-tuple-element.312.q_ref.k_ref.v_ref, ...), custom_call_target="tpu_custom_call" | custom-call | flops 1 | bytes 1 | tf_op jit(solution)/shard_map/attend_back/pallas_call | solution.py:310
  225.1 3.4 collective-permute-done.18.b
  229.8 3.6 all-to-all-start.2
  233.4 2.4 choose.1
  236.7 4.2 %add_convert_fusion = (bf16[256,1280]{1,0:T(8,128)(2,1)S(1)}, bf16[256,1280]{1,0:T(8,128)(2,1)S(1)}, bf16[256,1280]{1,0:T(8,128)(2,1)}, bf16[256,1280]{1,0:T(8,128)(2,1)}) fusion(bf16[1024,1280]{1,0:T(8,128)(2,1)} %collective-permute-done.17, bf16[1024,1280]{1,0:T(8,128)(2,1)} %get-tuple-element.322), kind=kLoop, calls=%fused_computation.1 | loop fusion | flops 5242880 | bytes 7864320 | tf_op jit(solution)/shard_map/convert_element_type | solution.py:848
  240.9 9.7 %qkv_grad.1.qkv_ref = bf16[1024,384]{1,0:T(8,128)(2,1)} custom-call(s32[1]{0:T(128)} %bitcast.1.core, bf16[1024,2048]{1,0:T(8,128)(2,1)} %get-tuple-element.248.h, bf16[1024,2048]{1,0:T(8,128)(2,1)} %collective-permute-done.6.h_other, bf16[2048,384]{1,0:T(8,128)(2,1)} %attend_back.2.refs_0_, bf16[2048,384]{1,0:T(8,128)(2,1)} %attend_back.3.refs_1_, ...), custom_call_target="tpu_custom_call" | custom-call | flops 1 | bytes 1 | tf_op jit(solution)/shard_map/qkv_grad/pallas_call | solution.py:721
  250.6 2.1 all-to-all-done.2
  256.2 2.9 collective-permute-start.22
  259.1 13.5 %join.1 = (bf16[512,1024]{1,0:T(8,128)(2,1)}, bf16[512,512]{1,0:T(8,128)(2,1)}, bf16[1024,512]{1,0:T(8,128)(2,1)}, f32[1,1024]{1,0:T(1,128)}, f32[1,1024]{1,0:T(1,128)}) custom-call(s32[1]{0:T(128)} %bitcast.1.core, bf16[2048,384]{1,0:T(8,128)(2,1)} %bitcast.47, bf16[2048,384]{1,0:T(8,128)(2,1)} %bitcast.48, bf16[1024,3072]{1,0:T(8,128)(2,1)} %wv.1, ...), custom_call_target="tpu_custom_call" | custom-call | flops 1 | bytes 1 | tf_op jit(solution)/shard_map/join/pallas_call | solution.py:832
  279.5 6.6 %aggregate_back.1 = (bf16[4,48,512]{2,1,0:T(8,128)(2,1)}, bf16[256,640]{1,0:T(8,128)(2,1)}, bf16[256,640]{1,0:T(8,128)(2,1)}) custom-call(s32[1]{0:T(128)} %bitcast.member, s32[1]{0:T(128)} %bitcast.1.core, s32[1]{0:T(128)S(6)} %copy.56.bucket, f32[4,48,2048]{2,1,0:T(8,128)} %get-tuple-element.238.pixel_ref, f32[5,48,128]{2,1,0:T(8,128)} %get-tuple-element.239.key_ref, ...), custom_call_target="tpu_custom_call" | custom-call | flops 1 | bytes 1 | tf_op jit(solution)/shard_map/aggregate_back/pallas_call | solution.py:408
  291.3 2.2 collective-permute-start.32
  293.5 5.1 %last_grad.1 = bf16[4,256,896]{2,1,0:T(8,128)(2,1)} custom-call(s32[1]{0:T(128)} %bitcast.1.core, bf16[1024,384]{1,0:T(8,128)(2,1)} %qkv_grad.1.qkv_ref, bf16[1024,512]{1,0:T(8,128)(2,1)} %get-tuple-element.249.a, bf16[1024,512]{1,0:T(8,128)(2,1)} %copy-done.14, bf16[512,1024]{1,0:T(8,128)(2,1)} %get-tuple-element.367.g, bf16[512,512]{1,0:T(8,128)(2,1)} %copy-done.22), custom_call_target="tpu_custom_call" | custom-call | flops 1 | bytes 1 | tf_op jit(solution)/shard_map/last_grad/pallas_call | solution.py:753
  300.3 2.9 collective-permute-done.31
  303.9 3.8 all-to-all-start.3
  310.7 4.6 %collective-permute-start.36 = (bf16[512,512]{1,0:T(8,128)(2,1)S(1)}, bf16[512,512]{1,0:T(8,128)(2,1)S(1)}, u32[]{:S(2)}, u32[]{:S(2)}) collective-permute-start(bf16[512,512]{1,0:T(8,128)(2,1)S(1)} %pad_maximum_fusion.1.refs_0_), channel_id=1, source_target_pairs={{0,2},{2,0},{4,6},{6,4},{1,3},{3,1},{5,7},{7,5},{8,10},{10,8},{12,... | collective-permute-start | bytes 1572872 | tf_op jit(solution)/shard_map/ppermute | solution.py:1051
  315.4 13.5 %all-to-all-done.3.came_ref = bf16[4,256,896]{2,1,0:T(8,128)(2,1)S(1)} async-done(((bf16[4,256,896]{2,1,0:T(8,128)(2,1)}), bf16[4,256,896]{2,1,0:T(8,128)(2,1)S(1)}, u32[]{:S(2)}, u32[]{:S(2)}) %all-to-all-start.3) | async-done | bytes 1835040 | tf_op jit(solution)/shard_map/all_to_all | solution.py:1059
  330.1 2.6 gather_sources.1
  332.8 2.0 collective-permute-start.35
  334.9 4.2 %collective-permute-done.35 = bf16[64,640]{1,0:T(8,128)(2,1)S(1)} collective-permute-done((bf16[64,640]{1,0:T(8,128)(2,1)S(1)}, bf16[64,640]{1,0:T(8,128)(2,1)S(1)}, u32[]{:S(2)}, u32[]{:S(2)}) %collective-permute-start.35) | collective-permute-done | bytes 81952 | tf_op jit(solution)/shard_map/ppermute | solution.py:1051
  340.3 3.4 collective-permute-start.40
  344.7 4.6 %assemble.3 = f32[1024,1024]{1,0:T(8,128)} custom-call(s32[2]{0:T(128)} %pad_add_fusion.1.where, bf16[512,512]{1,0:T(8,128)(2,1)} %copy-done.8, bf16[512,512]{1,0:T(8,128)(2,1)} %copy-done.23, bf16[512,512]{1,0:T(8,128)(2,1)} %copy-done.24, bf16[512,512]{1,0:T(8,128)(2,1)} %copy-done.25), custom_call_target="tpu_custom_call" | custom-call | flops 1 | bytes 1 | tf_op jit(solution)/shard_map/assemble/pallas_call | solution.py:952
  349.3 7.2 %collective-permute-done.40 = bf16[128,2048]{1,0:T(8,128)(2,1)S(1)} collective-permute-done((bf16[128,2048]{1,0:T(8,128)(2,1)}, bf16[128,2048]{1,0:T(8,128)(2,1)S(1)}, u32[]{:S(2)}, u32[]{:S(2)}) %collective-permute-start.40) | collective-permute-done | bytes 524320 | tf_op jit(solution)/shard_map/ppermute | solution.py:1051
  361.3 2.3 collective-permute-start.44
  368.0 6.2 %finish_tail.1 = (f32[256,1024]{1,0:T(8,128)}, f32[256,1024]{1,0:T(8,128)}, f32[1,256]{1,0:T(1,128)}, f32[12,4,1024]{2,1,0:T(4,128)}, f32[12,1024]{1,0:T(8,128)}) custom-call(s32[1]{0:T(128)} %bitcast.member, bf16[64,1152]{1,0:T(8,128)(2,1)} %copy-done.20, bf16[64,1152]{1,0:T(8,128)(2,1)} %copy-done.37, bf16[64,1152]{1,0:T(8,128)(2,1)} %collective-permute-done.42.refs_2_, ...), custom_call_target="tpu_custom_call" | custom-call | flops 1 | bytes 1 | tf_op jit(solution)/shard_map/finish_tail/pallas_call | solution.py:1030
  375.2 2.4 collective-permute-start.48
  383.2 2.0 collective-permute-done.47.refs_3_
  387.6 2.6 collective-permute-done.48
  393.5 5.0 %assemble.4 = (f32[256,4096]{1,0:T(8,128)}, f32[256,1024]{1,0:T(8,128)}) custom-call(s32[2]{0:T(128)} %pad_add_fusion.1.where, bf16[256,1280]{1,0:T(8,128)(2,1)} %copy-done.4, bf16[256,1280]{1,0:T(8,128)(2,1)} %copy-done.18, bf16[256,1280]{1,0:T(8,128)(2,1)} %copy-done.19, bf16[256,1280]{1,0:T(8,128)(2,1)} %collective-permute-done.51.refs_3_), custom_call_target="tpu_custom_call" | custom-call | flops 1 | bytes 1 | tf_op jit(solution)/shard_map/assemble/pallas_call | solution.py:952
  398.5 6.3 %collective-permute-done.52.refs_1_ = bf16[128,2048]{1,0:T(8,128)(2,1)} collective-permute-done((bf16[128,2048]{1,0:T(8,128)(2,1)S(1)}, bf16[128,2048]{1,0:T(8,128)(2,1)}, u32[]{:S(2)}, u32[]{:S(2)}) %collective-permute-start.52) | collective-permute-done | bytes 524320 | tf_op jit(solution)/shard_map/ppermute | solution.py:1051
  410.6 4.7 %assemble.5 = (f32[256,3072]{1,0:T(8,128)}, f32[256,1024]{1,0:T(8,128)}) custom-call(s32[2]{0:T(128)} %pad_add_fusion.1.where, bf16[128,2048]{1,0:T(8,128)(2,1)} %copy-done.9, bf16[128,2048]{1,0:T(8,128)(2,1)} %collective-permute-done.52.refs_1_, bf16[128,2048]{1,0:T(8,128)(2,1)} %copy-done.26, bf16[128,2048]{1,0:T(8,128)(2,1)} %copy-done.27), custom_call_target="tpu_custom_call" | custom-call | flops 1 | bytes 1 | tf_op jit(solution)/shard_map/assemble/pallas_call | solution.py:952
  (240 shorter events, 74.3 us)
Async XLA Ops:
  1.8 20.0 %collective-permute-start = (bf16[12,4,3072]{2,1,0:T(4,128)(2,1)S(1)}, bf16[12,4,3072]{2,1,0:T(4,128)(2,1)}, u32[]{:S(2)}, u32[]{:S(2)}) collective-permute-start(bf16[12,4,3072]{2,1,0:T(4,128)(2,1)S(1)} %pad_maximum_fusion.3.refs_0_), channel_id=1, source_target_pairs={{0,8},{8,0},{16,24},{24,16},{1,9},{9,1},{17,25},{25,17},{2,10},{10... | collective-permute-start | bytes 884744 | tf_op jit(solution)/shard_map/ppermute | solution.py:1051
  4.8 17.0 %collective-permute-start.1 = (bf16[12,4,3072]{2,1,0:T(4,128)(2,1)S(1)}, bf16[12,4,3072]{2,1,0:T(4,128)(2,1)}, u32[]{:S(2)}, u32[]{:S(2)}) collective-permute-start(bf16[12,4,3072]{2,1,0:T(4,128)(2,1)S(1)} %pad_maximum_fusion.3.refs_0_), channel_id=1, source_target_pairs={{0,16},{8,24},{16,0},{24,8},{1,17},{9,25},{17,1},{25,9},{2,18},{10... | collective-permute-start | bytes 884744 | tf_op jit(solution)/shard_map/ppermute | solution.py:1051
  6.3 15.5 %collective-permute-start.2 = (bf16[12,4,3072]{2,1,0:T(4,128)(2,1)S(1)}, bf16[12,4,3072]{2,1,0:T(4,128)(2,1)}, u32[]{:S(2)}, u32[]{:S(2)}) collective-permute-start(bf16[12,4,3072]{2,1,0:T(4,128)(2,1)S(1)} %pad_maximum_fusion.3.refs_0_), channel_id=1, source_target_pairs={{0,24},{8,16},{16,8},{24,0},{1,25},{9,17},{17,9},{25,1},{2,26},{10... | collective-permute-start | bytes 884744 | tf_op jit(solution)/shard_map/ppermute | solution.py:1051
  7.4 14.4 %collective-permute-start.3 = (bf16[512,512]{1,0:T(8,128)(2,1)S(1)}, bf16[512,512]{1,0:T(8,128)(2,1)S(1)}, u32[]{:S(2)}, u32[]{:S(2)}) collective-permute-start(bf16[512,512]{1,0:T(8,128)(2,1)S(1)} %dynamic-slice_bitcast_fusion), channel_id=1, source_target_pairs={{0,1},{1,0},{2,3},{3,2},{4,5},{5,4},{6,7},{7,6},{8,9},{9,8},{10,11... | collective-permute-start | bytes 1572872 | tf_op jit(solution)/shard_map/ppermute | solution.py:1051
  51.3 20.2 %collective-permute-start.6 = (bf16[1024,2048]{1,0:T(8,128)(2,1)}, bf16[1024,2048]{1,0:T(8,128)(2,1)}, u32[]{:S(2)}, u32[]{:S(2)}) collective-permute-start(bf16[1024,2048]{1,0:T(8,128)(2,1)} %get-tuple-element.248.h), channel_id=1, source_target_pairs={{0,1},{1,0},{2,3},{3,2},{4,5},{5,4},{6,7},{7,6},{8,9},{9,8},{10,11... | collective-permute-start | bytes 12582920 | tf_op jit(solution)/shard_map/ppermute | solution.py:1051
  51.8 19.7 %collective-permute-start.7 = (bf16[1024,512]{1,0:T(8,128)(2,1)}, bf16[1024,512]{1,0:T(8,128)(2,1)S(1)}, u32[]{:S(2)}, u32[]{:S(2)}) collective-permute-start(bf16[1024,512]{1,0:T(8,128)(2,1)} %get-tuple-element.249.a), channel_id=1, source_target_pairs={{0,1},{1,0},{2,3},{3,2},{4,5},{5,4},{6,7},{7,6},{8,9},{9,8},{10,11... | collective-permute-start | bytes 3145736 | tf_op jit(solution)/shard_map/ppermute | solution.py:1051
  59.7 10.8 %collective-permute-start.4 = (bf16[512,256]{1,0:T(8,128)(2,1)}, bf16[512,256]{1,0:T(8,128)(2,1)S(1)}, u32[]{:S(2)}, u32[]{:S(2)}) collective-permute-start(bf16[512,256]{1,0:T(8,128)(2,1)} %get-tuple-element.245.refs_3_), channel_id=1, source_target_pairs={{0,24},{8,16},{16,8},{24,0},{1,25},{9,17},{17,9},{25,1},{2,26},{10... | collective-permute-start | bytes 786440 | tf_op jit(solution)/shard_map/ppermute | solution.py:1051
  70.5 9.2 %collective-permute-start.5 = (bf16[512,256]{1,0:T(8,128)(2,1)}, bf16[512,256]{1,0:T(8,128)(2,1)S(1)}, u32[]{:S(2)}, u32[]{:S(2)}) collective-permute-start(bf16[512,256]{1,0:T(8,128)(2,1)} %get-tuple-element.247.refs_2_), channel_id=1, source_target_pairs={{0,16},{8,24},{16,0},{24,8},{1,17},{9,25},{17,1},{25,9},{2,18},{10... | collective-permute-start | bytes 786440 | tf_op jit(solution)/shard_map/ppermute | solution.py:1051
  79.7 10.6 %collective-permute-start.8 = (bf16[512,256]{1,0:T(8,128)(2,1)}, bf16[512,256]{1,0:T(8,128)(2,1)S(1)}, u32[]{:S(2)}, u32[]{:S(2)}) collective-permute-start(bf16[512,256]{1,0:T(8,128)(2,1)} %get-tuple-element.253.refs_1_), channel_id=1, source_target_pairs={{0,8},{8,0},{16,24},{24,16},{1,9},{9,1},{17,25},{25,17},{2,10},{10... | collective-permute-start | bytes 786440 | tf_op jit(solution)/shard_map/ppermute | solution.py:1051
  112.2 22.0 %collective-permute-start.9 = (bf16[4096,512]{1,0:T(8,128)(2,1)}, bf16[4096,512]{1,0:T(8,128)(2,1)}, u32[]{:S(2)}, u32[]{:S(2)}) collective-permute-start(bf16[4096,512]{1,0:T(8,128)(2,1)} %get-tuple-element.282.left), channel_id=1, source_target_pairs={{0,1},{1,0},{2,3},{3,2},{4,5},{5,4},{6,7},{7,6},{8,9},{9,8},{10,11... | collective-permute-start | bytes 12582920 | tf_op jit(solution)/shard_map/ppermute | solution.py:1051
  112.3 21.9 %collective-permute-start.10 = (bf16[512,2048]{1,0:T(8,128)(2,1)}, bf16[512,2048]{1,0:T(8,128)(2,1)S(1)}, u32[]{:S(2)}, u32[]{:S(2)}) collective-permute-start(bf16[512,2048]{1,0:T(8,128)(2,1)} %get-tuple-element.268.send_ref), channel_id=1, source_target_pairs={{0,1},{1,0},{2,3},{3,2},{4,5},{5,4},{6,7},{7,6},{8,9},{9,8},{10,11... | collective-permute-start | bytes 6291464 | tf_op jit(solution)/shard_map/ppermute | solution.py:1051
  112.8 21.4 %collective-permute-start.11 = (bf16[1024,512]{1,0:T(8,128)(2,1)}, bf16[1024,512]{1,0:T(8,128)(2,1)S(1)}, u32[]{:S(2)}, u32[]{:S(2)}) collective-permute-start(bf16[1024,512]{1,0:T(8,128)(2,1)} %get-tuple-element.269.h), channel_id=1, source_target_pairs={{0,1},{1,0},{2,3},{3,2},{4,5},{5,4},{6,7},{7,6},{8,9},{9,8},{10,11... | collective-permute-start | bytes 3145736 | tf_op jit(solution)/shard_map/ppermute | solution.py:1051
  112.8 21.3 %collective-permute-start.12 = (bf16[1024,512]{1,0:T(8,128)(2,1)}, bf16[1024,512]{1,0:T(8,128)(2,1)}, u32[]{:S(2)}, u32[]{:S(2)}) collective-permute-start(bf16[1024,512]{1,0:T(8,128)(2,1)} %get-tuple-element.270.m), channel_id=1, source_target_pairs={{0,1},{1,0},{2,3},{3,2},{4,5},{5,4},{6,7},{7,6},{8,9},{9,8},{10,11... | collective-permute-start | bytes 3145736 | tf_op jit(solution)/shard_map/ppermute | solution.py:1051
  134.2 4.9 %collective-permute-start.13 = (bf16[512,512]{1,0:T(8,128)(2,1)}, bf16[512,512]{1,0:T(8,128)(2,1)}, u32[]{:S(2)}, u32[]{:S(2)}) collective-permute-start(bf16[512,512]{1,0:T(8,128)(2,1)} %get-tuple-element.279), channel_id=1, source_target_pairs={{0,1},{1,0},{2,3},{3,2},{4,5},{5,4},{6,7},{7,6},{8,9},{9,8},{10,11... | collective-permute-start | bytes 1572872 | tf_op jit(solution)/shard_map/ppermute | solution.py:1051
  135.2 28.6 %all-to-all-start = ((bf16[4,512,256]{2,1,0:T(8,128)(2,1)}), bf16[4,512,256]{2,1,0:T(8,128)(2,1)S(1)}, u32[]{:S(2)}, u32[]{:S(2)}) async-start(bf16[4,512,256]{2,1,0:T(8,128)(2,1)} %get-tuple-element.291), calls=%async_computation | async-start | bytes 2097152 | tf_op jit(solution)/shard_map/all_to_all | solution.py:1059
  148.7 41.3 %collective-permute-start.14 = (bf16[1024,512]{1,0:T(8,128)(2,1)}, bf16[1024,512]{1,0:T(8,128)(2,1)}, u32[]{:S(2)}, u32[]{:S(2)}) collective-permute-start(bf16[1024,512]{1,0:T(8,128)(2,1)} %get-tuple-element.304), channel_id=1, source_target_pairs={{0,16},{8,24},{16,0},{24,8},{1,17},{9,25},{17,1},{25,9},{2,18},{10... | collective-permute-start | bytes 3145736 | tf_op jit(solution)/shard_map/ppermute | solution.py:1051
  150.7 39.3 %collective-permute-start.15 = (bf16[1024,512]{1,0:T(8,128)(2,1)}, bf16[1024,512]{1,0:T(8,128)(2,1)}, u32[]{:S(2)}, u32[]{:S(2)}) collective-permute-start(bf16[1024,512]{1,0:T(8,128)(2,1)} %get-tuple-element.305), channel_id=1, source_target_pairs={{0,8},{8,0},{16,24},{24,16},{1,9},{9,1},{17,25},{25,17},{2,10},{10... | collective-permute-start | bytes 3145736 | tf_op jit(solution)/shard_map/ppermute | solution.py:1051
  163.7 64.8 %collective-permute-start.17 = (bf16[1024,1280]{1,0:T(8,128)(2,1)}, bf16[1024,1280]{1,0:T(8,128)(2,1)}, u32[]{:S(2)}, u32[]{:S(2)}) collective-permute-start(bf16[1024,1280]{1,0:T(8,128)(2,1)} %get-tuple-element.313), channel_id=1, source_target_pairs={{0,2},{2,0},{4,6},{6,4},{1,3},{3,1},{5,7},{7,5},{8,10},{10,8},{12,... | collective-permute-start | bytes 7864328 | tf_op jit(solution)/shard_map/ppermute | solution.py:1051
  193.3 35.3 %collective-permute-start.16 = (bf16[2048,384]{1,0:T(8,128)(2,1)}, bf16[2048,384]{1,0:T(8,128)(2,1)S(1)}, u32[]{:S(2)}, u32[]{:S(2)}) collective-permute-start(bf16[2048,384]{1,0:T(8,128)(2,1)} %attend_back.2.refs_0_), channel_id=1, source_target_pairs={{0,1},{1,0},{2,3},{3,2},{4,5},{5,4},{6,7},{7,6},{8,9},{9,8},{10,11... | collective-permute-start | bytes 4718600 | tf_op jit(solution)/shard_map/ppermute | solution.py:1051
  193.3 35.2 %all-to-all-start.1 = ((bf16[4,512,384]{2,1,0:T(8,128)(2,1)}), bf16[4,512,384]{2,1,0:T(8,128)(2,1)S(1)}, u32[]{:S(2)}, u32[]{:S(2)}) async-start(bf16[4,512,384]{2,1,0:T(8,128)(2,1)} %bitcast.13), calls=%async_computation.1 | async-start | bytes 3145728 | tf_op jit(solution)/shard_map/all_to_all | solution.py:1059
  197.0 31.5 %collective-permute-start.18 = (bf16[512,512]{1,0:T(8,128)(2,1)}, bf16[512,512]{1,0:T(8,128)(2,1)}, u32[]{:S(2)}, u32[]{:S(2)}) collective-permute-start(bf16[512,512]{1,0:T(8,128)(2,1)} %get-tuple-element.314), channel_id=1, source_target_pairs={{0,8},{8,0},{16,24},{24,16},{1,9},{9,1},{17,25},{25,17},{2,10},{10... | collective-permute-start | bytes 1572872 | tf_op jit(solution)/shard_map/ppermute | solution.py:1051
  199.1 29.4 %collective-permute-start.19 = (bf16[512,512]{1,0:T(8,128)(2,1)}, bf16[512,512]{1,0:T(8,128)(2,1)}, u32[]{:S(2)}, u32[]{:S(2)}) collective-permute-start(bf16[512,512]{1,0:T(8,128)(2,1)} %get-tuple-element.315), channel_id=1, source_target_pairs={{0,16},{8,24},{16,0},{24,8},{1,17},{9,25},{17,1},{25,9},{2,18},{10... | collective-permute-start | bytes 1572872 | tf_op jit(solution)/shard_map/ppermute | solution.py:1051
  228.6 12.3 %collective-permute-start.20 = (bf16[2048,384]{1,0:T(8,128)(2,1)}, bf16[2048,384]{1,0:T(8,128)(2,1)}, u32[]{:S(2)}, u32[]{:S(2)}) collective-permute-start(bf16[2048,384]{1,0:T(8,128)(2,1)} %attend_back.3.refs_1_), channel_id=1, source_target_pairs={{0,1},{1,0},{2,3},{3,2},{4,5},{5,4},{6,7},{7,6},{8,9},{9,8},{10,11... | collective-permute-start | bytes 4718600 | tf_op jit(solution)/shard_map/ppermute | solution.py:1051
  229.8 23.0 %all-to-all-start.2 = ((bf16[4,512,384]{2,1,0:T(8,128)(2,1)}), bf16[4,512,384]{2,1,0:T(8,128)(2,1)S(1)}, u32[]{:S(2)}, u32[]{:S(2)}) async-start(bf16[4,512,384]{2,1,0:T(8,128)(2,1)} %bitcast.42), calls=%async_computation.2 | async-start | bytes 3145728 | tf_op jit(solution)/shard_map/all_to_all | solution.py:1059
  235.8 16.9 %collective-permute-start.21 = (bf16[512,512]{1,0:T(8,128)(2,1)}, bf16[512,512]{1,0:T(8,128)(2,1)}, u32[]{:S(2)}, u32[]{:S(2)}) collective-permute-start(bf16[512,512]{1,0:T(8,128)(2,1)} %get-tuple-element.328), channel_id=1, source_target_pairs={{0,2},{2,0},{4,6},{6,4},{1,3},{3,1},{5,7},{7,5},{8,10},{10,8},{12,... | collective-permute-start | bytes 1572872 | tf_op jit(solution)/shard_map/ppermute | solution.py:1051
  254.2 18.5 %collective-permute-start.23 = (bf16[256,1280]{1,0:T(8,128)(2,1)}, bf16[256,1280]{1,0:T(8,128)(2,1)}, u32[]{:S(2)}, u32[]{:S(2)}) collective-permute-start(bf16[256,1280]{1,0:T(8,128)(2,1)} %get-tuple-element.340), channel_id=1, source_target_pairs={{0,16},{8,24},{16,0},{24,8},{1,17},{9,25},{17,1},{25,9},{2,18},{10... | collective-permute-start | bytes 1966088 | tf_op jit(solution)/shard_map/ppermute | solution.py:1051
  255.7 16.9 %collective-permute-start.24 = (bf16[256,1280]{1,0:T(8,128)(2,1)}, bf16[256,1280]{1,0:T(8,128)(2,1)}, u32[]{:S(2)}, u32[]{:S(2)}) collective-permute-start(bf16[256,1280]{1,0:T(8,128)(2,1)} %get-tuple-element.341), channel_id=1, source_target_pairs={{0,8},{8,0},{16,24},{24,16},{1,9},{9,1},{17,25},{25,17},{2,10},{10... | collective-permute-start | bytes 1966088 | tf_op jit(solution)/shard_map/ppermute | solution.py:1051
  256.2 16.4 %collective-permute-start.22 = (bf16[256,512]{1,0:T(8,128)(2,1)S(1)}, bf16[256,512]{1,0:T(8,128)(2,1)S(1)}, u32[]{:S(2)}, u32[]{:S(2)}) collective-permute-start(bf16[256,512]{1,0:T(8,128)(2,1)S(1)} %add_convert_fusion.20), channel_id=1, source_target_pairs={{0,6},{2,4},{4,2},{6,0},{1,7},{3,5},{5,3},{7,1},{8,14},{10,12},{12... | collective-permute-start | bytes 786440 | tf_op jit(solution)/shard_map/ppermute | solution.py:1051
  276.0 11.4 %collective-permute-start.25 = (bf16[512,512]{1,0:T(8,128)(2,1)}, bf16[512,512]{1,0:T(8,128)(2,1)S(1)}, u32[]{:S(2)}, u32[]{:S(2)}) collective-permute-start(bf16[512,512]{1,0:T(8,128)(2,1)} %get-tuple-element.354), channel_id=1, source_target_pairs={{0,1},{1,0},{2,3},{3,2},{4,5},{5,4},{6,7},{7,6},{8,9},{9,8},{10,11... | collective-permute-start | bytes 1572872 | tf_op jit(solution)/shard_map/ppermute | solution.py:1051
  276.1 10.1 %collective-permute-start.26 = (bf16[128,1280]{1,0:T(8,128)(2,1)S(1)}, bf16[128,1280]{1,0:T(8,128)(2,1)S(1)}, u32[]{:S(2)}, u32[]{:S(2)}) collective-permute-start(bf16[128,1280]{1,0:T(8,128)(2,1)S(1)} %add_convert_fusion.15), channel_id=1, source_target_pairs={{0,8},{8,0},{16,24},{24,16},{1,9},{9,1},{17,25},{25,17},{2,10},{10... | collective-permute-start | bytes 983048 | tf_op jit(solution)/shard_map/ppermute | solution.py:1051
  277.6 9.8 %collective-permute-start.27 = (bf16[128,1280]{1,0:T(8,128)(2,1)S(1)}, bf16[128,1280]{1,0:T(8,128)(2,1)S(1)}, u32[]{:S(2)}, u32[]{:S(2)}) collective-permute-start(bf16[128,1280]{1,0:T(8,128)(2,1)S(1)} %add_convert_fusion.14), channel_id=1, source_target_pairs={{0,16},{8,24},{16,0},{24,8},{1,17},{9,25},{17,1},{25,9},{2,18},{10... | collective-permute-start | bytes 983048 | tf_op jit(solution)/shard_map/ppermute | solution.py:1051
  278.2 20.4 %collective-permute-start.30 = (bf16[256,512]{1,0:T(8,128)(2,1)S(1)}, bf16[256,512]{1,0:T(8,128)(2,1)}, u32[]{:S(2)}, u32[]{:S(2)}) collective-permute-start(bf16[256,512]{1,0:T(8,128)(2,1)S(1)} %add_convert_fusion.19), channel_id=1, source_target_pairs={{0,6},{2,4},{4,2},{6,0},{1,7},{3,5},{5,3},{7,1},{8,14},{10,12},{12... | collective-permute-start | bytes 786440 | tf_op jit(solution)/shard_map/ppermute | solution.py:1051
  290.7 7.8 %collective-permute-start.29 = (bf16[128,640]{1,0:T(8,128)(2,1)S(1)}, bf16[128,640]{1,0:T(8,128)(2,1)S(1)}, u32[]{:S(2)}, u32[]{:S(2)}) collective-permute-start(bf16[128,640]{1,0:T(8,128)(2,1)S(1)} %slice.138), channel_id=1, source_target_pairs={{0,8},{8,0},{16,24},{24,16},{1,9},{9,1},{17,25},{25,17},{2,10},{10... | collective-permute-start | bytes 491528 | tf_op jit(solution)/shard_map/ppermute | solution.py:1051
  291.3 11.8 %collective-permute-start.32 = (bf16[128,1280]{1,0:T(8,128)(2,1)S(1)}, bf16[128,1280]{1,0:T(8,128)(2,1)S(1)}, u32[]{:S(2)}, u32[]{:S(2)}) collective-permute-start(bf16[128,1280]{1,0:T(8,128)(2,1)S(1)} %fusion.3), channel_id=1, source_target_pairs={{0,6},{2,4},{4,2},{6,0},{1,7},{3,5},{5,3},{7,1},{8,14},{10,12},{12... | collective-permute-start | bytes 983048 | tf_op jit(solution)/shard_map/ppermute | solution.py:1051
  303.9 25.0 %all-to-all-start.3 = ((bf16[4,256,896]{2,1,0:T(8,128)(2,1)}), bf16[4,256,896]{2,1,0:T(8,128)(2,1)S(1)}, u32[]{:S(2)}, u32[]{:S(2)}) async-start(bf16[4,256,896]{2,1,0:T(8,128)(2,1)} %last_grad.1), calls=%async_computation.3 | async-start | bytes 3670016 | tf_op jit(solution)/shard_map/all_to_all | solution.py:1059
  309.0 23.7 %collective-permute-start.34 = (bf16[128,1280]{1,0:T(8,128)(2,1)S(1)}, bf16[128,1280]{1,0:T(8,128)(2,1)}, u32[]{:S(2)}, u32[]{:S(2)}) collective-permute-start(bf16[128,1280]{1,0:T(8,128)(2,1)S(1)} %add_convert_fusion.8), channel_id=1, source_target_pairs={{0,6},{2,4},{4,2},{6,0},{1,7},{3,5},{5,3},{7,1},{8,14},{10,12},{12... | collective-permute-start | bytes 983048 | tf_op jit(solution)/shard_map/ppermute | solution.py:1051
  310.7 24.1 %collective-permute-start.36 = (bf16[512,512]{1,0:T(8,128)(2,1)S(1)}, bf16[512,512]{1,0:T(8,128)(2,1)S(1)}, u32[]{:S(2)}, u32[]{:S(2)}) collective-permute-start(bf16[512,512]{1,0:T(8,128)(2,1)S(1)} %pad_maximum_fusion.1.refs_0_), channel_id=1, source_target_pairs={{0,2},{2,0},{4,6},{6,4},{1,3},{3,1},{5,7},{7,5},{8,10},{10,8},{12,... | collective-permute-start | bytes 1572872 | tf_op jit(solution)/shard_map/ppermute | solution.py:1051
  315.4 17.3 %collective-permute-start.33 = (bf16[64,640]{1,0:T(8,128)(2,1)S(1)}, bf16[64,640]{1,0:T(8,128)(2,1)S(1)}, u32[]{:S(2)}, u32[]{:S(2)}) collective-permute-start(bf16[64,640]{1,0:T(8,128)(2,1)S(1)} %add_convert_fusion.25), channel_id=1, source_target_pairs={{0,2},{2,0},{4,6},{6,4},{1,3},{3,1},{5,7},{7,5},{8,10},{10,8},{12,... | collective-permute-start | bytes 245768 | tf_op jit(solution)/shard_map/ppermute | solution.py:1051
  332.8 6.3 %collective-permute-start.35 = (bf16[64,640]{1,0:T(8,128)(2,1)S(1)}, bf16[64,640]{1,0:T(8,128)(2,1)S(1)}, u32[]{:S(2)}, u32[]{:S(2)}) collective-permute-start(bf16[64,640]{1,0:T(8,128)(2,1)S(1)} %add_convert_fusion.24), channel_id=1, source_target_pairs={{0,6},{2,4},{4,2},{6,0},{1,7},{3,5},{5,3},{7,1},{8,14},{10,12},{12... | collective-permute-start | bytes 245768 | tf_op jit(solution)/shard_map/ppermute | solution.py:1051
  340.3 16.1 %collective-permute-start.40 = (bf16[128,2048]{1,0:T(8,128)(2,1)}, bf16[128,2048]{1,0:T(8,128)(2,1)S(1)}, u32[]{:S(2)}, u32[]{:S(2)}) collective-permute-start(bf16[128,2048]{1,0:T(8,128)(2,1)} %get-tuple-element.400), channel_id=1, source_target_pairs={{0,2},{2,0},{4,6},{6,4},{1,3},{3,1},{5,7},{7,5},{8,10},{10,8},{12,... | collective-permute-start | bytes 1572872 | tf_op jit(solution)/shard_map/ppermute | solution.py:1051
  357.8 8.4 %collective-permute-start.41 = (bf16[64,1152]{1,0:T(8,128)(2,1)S(1)}, bf16[64,1152]{1,0:T(8,128)(2,1)S(1)}, u32[]{:S(2)}, u32[]{:S(2)}) collective-permute-start(bf16[64,1152]{1,0:T(8,128)(2,1)S(1)} %pad_maximum_fusion.4.refs_0_), channel_id=1, source_target_pairs={{0,8},{8,0},{16,24},{24,16},{1,9},{9,1},{17,25},{25,17},{2,10},{10... | collective-permute-start | bytes 442376 | tf_op jit(solution)/shard_map/ppermute | solution.py:1051
  359.3 8.7 %collective-permute-start.42 = (bf16[64,1152]{1,0:T(8,128)(2,1)S(1)}, bf16[64,1152]{1,0:T(8,128)(2,1)}, u32[]{:S(2)}, u32[]{:S(2)}) collective-permute-start(bf16[64,1152]{1,0:T(8,128)(2,1)S(1)} %pad_maximum_fusion.4.refs_0_), channel_id=1, source_target_pairs={{0,16},{8,24},{16,0},{24,8},{1,17},{9,25},{17,1},{25,9},{2,18},{10... | collective-permute-start | bytes 442376 | tf_op jit(solution)/shard_map/ppermute | solution.py:1051
  359.9 8.1 %collective-permute-start.43 = (bf16[64,1152]{1,0:T(8,128)(2,1)S(1)}, bf16[64,1152]{1,0:T(8,128)(2,1)}, u32[]{:S(2)}, u32[]{:S(2)}) collective-permute-start(bf16[64,1152]{1,0:T(8,128)(2,1)S(1)} %pad_maximum_fusion.4.refs_0_), channel_id=1, source_target_pairs={{0,24},{8,16},{16,8},{24,0},{1,25},{9,17},{17,9},{25,1},{2,26},{10... | collective-permute-start | bytes 442376 | tf_op jit(solution)/shard_map/ppermute | solution.py:1051
  361.3 12.8 %collective-permute-start.44 = (bf16[64,2048]{1,0:T(8,128)(2,1)S(1)}, bf16[64,2048]{1,0:T(8,128)(2,1)S(1)}, u32[]{:S(2)}, u32[]{:S(2)}) collective-permute-start(bf16[64,2048]{1,0:T(8,128)(2,1)S(1)} %add_convert_fusion.17), channel_id=1, source_target_pairs={{0,6},{2,4},{4,2},{6,0},{1,7},{3,5},{5,3},{7,1},{8,14},{10,12},{12... | collective-permute-start | bytes 786440 | tf_op jit(solution)/shard_map/ppermute | solution.py:1051
  365.3 24.9 %collective-permute-start.49 = (bf16[256,1280]{1,0:T(8,128)(2,1)S(1)}, bf16[256,1280]{1,0:T(8,128)(2,1)S(1)}, u32[]{:S(2)}, u32[]{:S(2)}) collective-permute-start(bf16[256,1280]{1,0:T(8,128)(2,1)S(1)} %pad_maximum_fusion.refs_0_), channel_id=1, source_target_pairs={{0,2},{2,0},{4,6},{6,4},{1,3},{3,1},{5,7},{7,5},{8,10},{10,8},{12,... | collective-permute-start | bytes 1966088 | tf_op jit(solution)/shard_map/ppermute | solution.py:1051
  375.2 15.0 %collective-permute-start.48 = (bf16[64,2048]{1,0:T(8,128)(2,1)S(1)}, bf16[64,2048]{1,0:T(8,128)(2,1)S(1)}, u32[]{:S(2)}, u32[]{:S(2)}) collective-permute-start(bf16[64,2048]{1,0:T(8,128)(2,1)S(1)} %add_convert_fusion.16), channel_id=1, source_target_pairs={{0,6},{2,4},{4,2},{6,0},{1,7},{3,5},{5,3},{7,1},{8,14},{10,12},{12... | collective-permute-start | bytes 786440 | tf_op jit(solution)/shard_map/ppermute | solution.py:1051
  380.0 5.2 %collective-permute-start.47 = (bf16[4,12,512]{2,1,0:T(8,128)(2,1)S(1)}, bf16[4,12,512]{2,1,0:T(8,128)(2,1)S(1)}, u32[]{:S(2)}, u32[]{:S(2)}) collective-permute-start(bf16[4,12,512]{2,1,0:T(8,128)(2,1)S(1)} %bitcast.55), channel_id=1, source_target_pairs={{0,24},{8,16},{16,8},{24,0},{1,25},{9,17},{17,9},{25,1},{2,26},{10... | collective-permute-start | bytes 147464 | tf_op jit(solution)/shard_map/ppermute | solution.py:1051
  390.8 14.0 %collective-permute-start.52 = (bf16[128,2048]{1,0:T(8,128)(2,1)S(1)}, bf16[128,2048]{1,0:T(8,128)(2,1)}, u32[]{:S(2)}, u32[]{:S(2)}) collective-permute-start(bf16[128,2048]{1,0:T(8,128)(2,1)S(1)} %pad_maximum_fusion.2.refs_0_), channel_id=1, source_target_pairs={{0,2},{2,0},{4,6},{6,4},{1,3},{3,1},{5,7},{7,5},{8,10},{10,8},{12,... | collective-permute-start | bytes 1572872 | tf_op jit(solution)/shard_map/ppermute | solution.py:1051
  (57 other events, 523.4 us)
